TPU v7x, 256 devices: a whole 4x4x8 slice. The times are simulated.
256 devices in a mesh: ep: 64 (over z, y, core), sp: 4 (over x).
Axes of the slice: x: 4, y: 4, z: 8, core: 2. Of those that a mesh axis runs over, the one named last changes fastest.
Arguments:
- stream: bfloat16 [32768, 4096], P(('ep', 'sp')), may hold values from -30 to 30
- query_base: bfloat16 [32768, 4096], P(('ep', 'sp')), may hold values from -40 to 40
- key_heads: bfloat16 [32768, 1024], P(('ep', 'sp')), may hold values from -6 to 6
- value_heads: bfloat16 [32768, 1024], P(('ep', 'sp')), may hold values from -12 to 12
- attention_gain: bfloat16 [4096], replicated, may hold values from 0.099609375 to 1.8984375
- expert_gain: bfloat16 [4096], replicated, may hold values from 0.099609375 to 1.8984375
- adapter_down: bfloat16 [4096, 128], P('sp'), may hold values from -0.09375 to 0.09375
- adapter_up: bfloat16 [4096, 128], P('sp'), may hold values from -1 to 1
- user_index: int32 [64], P('ep'), may hold values from 0 to 3
- routes: int32 [32768, 2], P('ep'), may hold values from 0 to 63, all different within a row; in each aligned block of 128 rows (0 to 127, 128 to 255, ...) at most 5 rows name the same one
- route_weights: int32 [32768, 2], P(('ep', 'sp')), may hold values from 1 to 4
- gate_weight: bfloat16 [64, 4096, 1536], P('ep', None, 'sp'), may hold values from -0.09375 to 0.09375
- up_weight: bfloat16 [64, 4096, 1536], P('ep', None, 'sp'), may hold values from -0.09375 to 0.09375
- down_weight: bfloat16 [64, 1536, 4096], P('ep', 'sp'), may hold values from -0.15625 to 0.15625
Outputs:
- hidden_state: bfloat16 [32768, 4096], P(('ep', 'sp'))
- moe_out: bfloat16 [32768, 4096], P(('ep', 'sp'))
Inputs may be any that keep to these rules, and one draw needn't show every extreme that they name: `routes`: each row names 2 different experts. In each aligned block of 128 rows (the tokens of one device) no expert is named more than 5 times, and in some block some expert is named exactly 5 times.
All inputs are finite; a program needn't handle non-finite values.
Results may differ from a plain program's by a relative error of at most 0.019.
Values may be sent and summed in bfloat16 or wider, within the bound.
No kernel may reach another device: no remote copies, remote signals or barrier semaphores. Data moves between devices by JAX's collectives and lax.ppermute only.
A program may use at most 128 MiB of HBM per device.

v0:
```python
import jax
import jax.numpy as jnp
from jax import lax
from jax.sharding import PartitionSpec as P

D = 4096
HEADS = 32
KV_HEADS = 8
HEAD = 128
RANK = 32


epsilon = 1e-06


def rms_scale(inputs, gain_vec):
    widened = inputs.astype(jnp.float32)
    return (
        widened
        * lax.rsqrt(jnp.mean(widened * widened, axis=-1, keepdims=True) + epsilon)
        * gain_vec.astype(jnp.float32)
    )


def route_slots(block_routes, experts):
    flat_routes = block_routes.reshape(-1)
    matches = (flat_routes[:, None] == jnp.arange(experts, dtype=jnp.int32)[None, :]).astype(
        jnp.int32
    )
    earlier = jnp.cumsum(matches, axis=0) - matches
    return (flat_routes, jnp.sum(earlier * matches, axis=1))


def attention_block(
    stream_rows, base_rows, key_rows, value_rows, user_id, attention_gain, adapter_down, adapter_up
):
    normed = rms_scale(stream_rows, attention_gain).astype(jnp.bfloat16)
    down_cols = lax.dynamic_slice_in_dim(adapter_down, user_id * RANK, RANK, 1)
    up_cols = lax.dynamic_slice_in_dim(adapter_up, user_id * RANK, RANK, 1)
    low_rank = jnp.dot(normed, down_cols, preferred_element_type=jnp.float32).astype(jnp.bfloat16)
    adapter_delta = jnp.dot(low_rank, up_cols.T, preferred_element_type=jnp.float32)
    queries = (base_rows.astype(jnp.float32) + adapter_delta).astype(jnp.bfloat16)
    group_size = HEADS // KV_HEADS
    row_total = queries.shape[0]
    query_heads = queries.reshape(row_total, KV_HEADS, group_size, HEAD)
    key_split = key_rows.reshape(-1, KV_HEADS, HEAD)
    value_split = value_rows.reshape(-1, KV_HEADS, HEAD)
    scores = jnp.einsum(
        "qhgd,khd->hgqk", query_heads, key_split, preferred_element_type=jnp.float32
    ) * HEAD ** (-0.5)
    row_max = jnp.max(scores, axis=-1, keepdims=True)
    exponent = jnp.exp(scores - row_max)
    attn_probs = (exponent / jnp.sum(exponent, axis=-1, keepdims=True)).astype(jnp.bfloat16)
    attended = jnp.einsum(
        "hgqk,khd->qhgd", attn_probs, value_split, preferred_element_type=jnp.float32
    ).reshape(row_total, D)
    return (stream_rows.astype(jnp.float32) + attended).astype(jnp.bfloat16)


def on_device(
    stream,
    query_base,
    key_heads,
    value_heads,
    attention_gain,
    expert_gain,
    adapter_down,
    adapter_up,
    user_index,
    routes,
    route_weights,
    gate_weight,
    up_weight,
    down_weight,
):
    key_all, value_all, down_all, up_all = (
        lax.all_gather(key_heads, "sp", axis=0, tiled=True),
        lax.all_gather(value_heads, "sp", axis=0, tiled=True),
        lax.all_gather(adapter_down, "sp", axis=0, tiled=True),
        lax.all_gather(adapter_up, "sp", axis=0, tiled=True),
    )
    hidden_state = attention_block(
        stream, query_base, key_all, value_all, user_index[0], attention_gain, down_all, up_all
    )
    normed_moe = rms_scale(hidden_state, expert_gain).astype(jnp.bfloat16)
    tokens_dev = stream.shape[0]
    top_count = routes.shape[1]
    model_width = stream.shape[1]
    experts = lax.axis_size("ep")
    capacity = max(2, (5 * tokens_dev * top_count + 4 * experts - 1) // (4 * experts))
    own_routes = lax.dynamic_slice_in_dim(routes, lax.axis_index("sp") * tokens_dev, tokens_dev, 0)
    flat_routes, slot_index = route_slots(own_routes, experts)
    position = flat_routes * capacity + slot_index
    padded = jnp.concatenate([normed_moe, jnp.zeros((1, model_width), jnp.bfloat16)], axis=0)
    token_ids = jnp.arange(tokens_dev * top_count, dtype=jnp.int32) // top_count
    slot_table = jnp.full((experts * capacity,), tokens_dev, jnp.int32).at[position].set(token_ids)
    outgoing = padded[slot_table].reshape(experts, capacity, model_width)
    received = lax.all_to_all(outgoing, "ep", split_axis=0, concat_axis=0, tiled=True)
    arrived = lax.all_gather(received, "sp", axis=0, tiled=True)
    all_rows = arrived.reshape(-1, model_width)
    gate_local = gate_weight[0]
    up_local = up_weight[0]
    down_local = down_weight[0]
    gate_out = jnp.dot(all_rows, gate_local, preferred_element_type=jnp.float32)
    up_out = jnp.dot(all_rows, up_local, preferred_element_type=jnp.float32)
    activated = (jax.nn.silu(gate_out) * up_out).astype(jnp.bfloat16)
    summed = lax.psum_scatter(
        jnp.dot(activated, down_local, preferred_element_type=jnp.float32).astype(jnp.bfloat16),
        "sp",
        scatter_dimension=0,
        tiled=True,
    )
    expert_out = summed.reshape(experts, capacity, model_width)
    returned = lax.all_to_all(expert_out, "ep", split_axis=0, concat_axis=0, tiled=True)
    picked = returned.reshape(experts * capacity, model_width)[position].reshape(
        tokens_dev, top_count, model_width
    )
    route_share = route_weights.astype(jnp.float32)
    route_share = route_share / jnp.sum(route_share, axis=1, keepdims=True)
    moe_out = jnp.sum(picked.astype(jnp.float32) * route_share[:, :, None], axis=1).astype(
        jnp.bfloat16
    )
    return (hidden_state, moe_out)


def solution(mesh):
    in_specs = (
        P(("ep", "sp"), None),
        P(("ep", "sp"), None),
        P(("ep", "sp"), None),
        P(("ep", "sp"), None),
        P(),
        P(),
        P("sp", None),
        P("sp", None),
        P("ep"),
        P("ep", None),
        P(("ep", "sp"), None),
        P("ep", None, "sp"),
        P("ep", None, "sp"),
        P("ep", "sp", None),
    )
    out_specs = (P(("ep", "sp"), None), P(("ep", "sp"), None))
    return jax.shard_map(
        on_device, mesh=mesh, in_specs=in_specs, out_specs=out_specs, check_vma=False
    )
```

profile of v0, /device:TPU:6, one launch (start us, length us, event | category | flops | bytes accessed | tf_op | source)
XLA Modules:
  0.0 678.4 jit_solution(350134085212804269)
XLA Ops:
  7.2 0.0 copy-start
  7.2 0.0 copy-start.3
  7.2 0.0 all-gather.6.cloned.1.call-start
  7.2 0.7 all-gather.6.cloned.1.call-update
  7.9 0.0 all-gather.8.cloned.1.call-start
  8.0 0.7 all-gather.8.cloned.1.call-update
  8.7 0.0 all-gather.10.cloned.1.call-start
  8.7 1.8 copy.30
  10.5 0.0 all-gather.10.cloned.1.call-update
  10.6 0.0 all-gather.12.cloned.1.call-start
  10.6 0.5 all-gather.12.cloned.1.call-update
  11.1 0.0 all-gather.14.cloned.1.call-start
  11.2 0.7 broadcast_multiply_fusion
  11.9 0.1 copy.36
  12.0 0.1 eq.29
  12.1 0.1 eq.25
  12.9 0.6 reduce-window.6
  13.6 0.2 slice_reduce_fusion
  13.8 0.1 copy.35
  13.9 0.1 mul.109
  14.0 0.1 fusion.44
  14.2 1.4 scatter_custom_fusion
  15.6 0.7 convert_element_type.61
  16.3 1.5 fusion.21
  17.8 20.5 %all-gather.6.cloned.1.call-done = bf16[4096,128]{1,0:T(8,128)(2,1)} async-done(((bf16[1024,128]{1,0:T(8,128)(2,1)}), bf16[4096,128]{1,0:T(8,128)(2,1)}) %all-gather.6.cloned.1.call-update) | async-done | bytes 1048592 | tf_op jit(solution)/shard_map/all_gather | solution.py:79
  38.4 28.7 %all-gather.8.cloned.1.call-done = bf16[4096,128]{1,0:T(8,128)(2,1)} async-done(((bf16[1024,128]{1,0:T(8,128)(2,1)}), bf16[4096,128]{1,0:T(8,128)(2,1)}) %all-gather.8.cloned.1.call-update) | async-done | bytes 1048592 | tf_op jit(solution)/shard_map/all_gather | solution.py:80
  67.1 4.9 fusion.6
  71.9 2.7 reshape.101
  74.7 23.3 %all-gather.10.cloned.1.call-done = bf16[512,1024]{0,1:T(8,128)(2,1)} async-done(((bf16[128,1024]{0,1:T(8,128)(2,1)}), bf16[512,1024]{0,1:T(8,128)(2,1)}) %all-gather.10.cloned.1.call-update) | async-done | bytes 1048592 | tf_op jit(solution)/shard_map/all_gather | solution.py:77
  97.9 2.8 fusion.32
  100.7 0.0 copy-start.1
  100.7 3.2 copy-done.1
  103.9 2.4 fusion.60
  106.4 20.5 %all-gather.12.cloned.1.call-done = bf16[512,1024]{1,0:T(8,128)(2,1)} async-done(((bf16[128,1024]{1,0:T(8,128)(2,1)}), bf16[512,1024]{1,0:T(8,128)(2,1)}) %all-gather.12.cloned.1.call-update) | async-done | bytes 1048592 | tf_op jit(solution)/shard_map/all_gather | solution.py:78
  126.9 2.3 copy.33
  129.1 12.1 %fusion.8 = f32[8,4,128,128]{2,3,1,0:T(8,128)} fusion(bf16[512,8,128,1]{0,2,3,1:T(8,128)(2,1)} %bitcast.73, f32[8,4,128]{2,1,0:T(4,128)S(1)} %fusion.60, f32[8,128,4,512]{3,1,2,0:T(8,128)} %copy-done.1), kind=kOutput, calls=%fused_computation.15 | convolution fusion | flops 547361280 | bytes 11550720 | tf_op jit(solution)/shard_map/hgqk,khd->qhgd/dot_general | solution.py:54
  141.3 2.9 copy.34
  144.2 2.3 fusion.18
  146.4 0.0 copy-start.2
  146.5 1.0 copy-done.2
  147.4 0.3 fusion.20
  147.8 1.1 concatenate.3
  148.9 9.5 %gather_fusion = bf16[320,4096]{1,0:T(8,128)(2,1)} fusion(bf16[129,4096]{1,0:T(8,128)(2,1)} %concatenate.3, s32[1024]{0:T(1024)S(1)} %pad_clamp_fusion.1), kind=kCustom, calls=%fused_computation | custom fusion | bytes 5244160 | tf_op jit(solution)/shard_map/gather | solution.py:97
  158.4 4.7 reshape.106
  163.1 107.0 %all_to_all.10 = bf16[64,5,4096]{2,1,0:T(8,128)(2,1)S(1)} all-to-all(bf16[64,5,4096]{2,1,0:T(8,128)(2,1)} %reshape.106), channel_id=1, replica_groups=mesh['ep'=64,'sp'=4] {'ep'}, dimensions={0} | all-to-all | bytes 5242880 | tf_op jit(solution)/shard_map/all_to_all | solution.py:98
  270.1 3.2 copy.39
  273.3 0.0 all-gather.14.cloned.1.call-update
  273.3 0.0 reduce-scatter.2.cloned.1.call-start
  273.3 98.5 %all-gather.14.cloned.1.call-done = bf16[256,5,4096]{2,0,1:T(8,128)(2,1)} async-done(((bf16[64,5,4096]{2,0,1:T(8,128)(2,1)}), bf16[256,5,4096]{2,0,1:T(8,128)(2,1)}) %all-gather.14.cloned.1.call-update) | async-done | bytes 10485776 | tf_op jit(solution)/shard_map/all_gather | solution.py:99
  371.8 15.2 %copy.40 = bf16[256,5,4096]{2,1,0:T(8,128)(2,1)} copy(bf16[256,5,4096]{2,0,1:T(8,128)(2,1)} %all-gather.14.cloned.1.call-done) | data formatting | bytes 20971520 | tf_op jit(solution)/shard_map/all_gather | solution.py:99
  387.1 16.8 %reshape.107 = bf16[1280,4096]{1,0:T(8,128)(2,1)} reshape(bf16[256,5,4096]{2,1,0:T(8,128)(2,1)} %copy.40) | data formatting | bytes 20971520 | tf_op jit(solution)/shard_map/reshape | solution.py:100
  403.9 10.1 %fusion.11 = f32[1280,384]{1,0:T(8,128)} fusion(bf16[1280,4096]{1,0:T(8,128)(2,1)} %reshape.107, bf16[1,4096,384]{2,1,0:T(8,128)(2,1)} %param.25), kind=kOutput, calls=%fused_computation.19 | convolution fusion | flops 4026531840 | bytes 15597568 | tf_op jit(solution)/shard_map/dot_general | solution.py:104
  414.0 0.0 copy-done
  414.0 17.3 %convolution_convert_fusion = bf16[1280,4096]{1,0:T(8,128)(2,1)} fusion(bf16[1,384,4096]{2,1,0:T(8,128)(2,1)S(1)} %copy-done, bf16[1280,4096]{1,0:T(8,128)(2,1)} %reshape.107, bf16[1,4096,384]{2,1,0:T(8,128)(2,1)} %param.26, f32[1280,384]{1,0:T(8,128)} %fusion.11), kind=kOutput, calls=%fused_computation.4 | convolution fusion | flops 8061255680 | bytes 29229056 | tf_op jit(solution)/shard_map/dot_general | solution.py:108
  431.4 0.0 reduce-scatter.2.cloned.1.call-update
  431.4 100.5 %reduce-scatter.2.cloned.1.call-done = bf16[320,4096]{1,0:T(8,128)(2,1)} async-done(((bf16[1280,4096]{1,0:T(8,128)(2,1)}), bf16[320,4096]{1,0:T(8,128)(2,1)}) %reduce-scatter.2.cloned.1.call-update) | async-done | bytes 2621456 | tf_op jit(solution)/shard_map/reduce_scatter | solution.py:107
  531.9 4.7 reshape.108
  536.6 11.1 %all-to-all-start.1 = ((bf16[64,5,4096]{2,1,0:T(8,128)(2,1)}), bf16[64,5,4096]{2,1,0:T(8,128)(2,1)}, u32[]{:S(2)}, u32[]{:S(2)}) async-start(bf16[64,5,4096]{2,1,0:T(8,128)(2,1)} %reshape.108), calls=%async_computation.2 | async-start | bytes 8388608 | tf_op jit(solution)/shard_map/all_to_all | solution.py:114
  547.7 0.1 copy.41
  547.9 96.0 %all-to-all-done.1 = bf16[64,5,4096]{2,1,0:T(8,128)(2,1)} async-done(((bf16[64,5,4096]{2,1,0:T(8,128)(2,1)}), bf16[64,5,4096]{2,1,0:T(8,128)(2,1)}, u32[]{:S(2)}, u32[]{:S(2)}) %all-to-all-start.1) | async-done | bytes 2621472 | tf_op jit(solution)/shard_map/all_to_all | solution.py:114
  643.9 4.8 reshape.109
  648.7 7.4 %gather_fusion.1 = bf16[256,4096]{1,0:T(8,128)(2,1)} fusion(bf16[320,4096]{1,0:T(8,128)(2,1)} %reshape.109, s32[1024]{0:T(1024)S(1)} %pad_clamp_fusion), kind=kCustom, calls=%fused_computation.1 | custom fusion | bytes 4195328 | tf_op jit(solution)/shard_map/gather | solution.py:115
  656.0 5.4 reshape.110
  661.5 9.6 %multiply_reduce_fusion = bf16[128,4096]{1,0:T(8,128)(2,1)} fusion(f32[128,2,4096]{2,1,0:T(2,128)} %reshape.110, f32[128,2]{1,0:T(8,128)S(1)} %copy.41), kind=kLoop, calls=%fused_computation.13 | loop fusion | flops 1572864 | bytes 5243904 | tf_op jit(solution)/shard_map/reduce_sum | solution.py:120
  (16 shorter events, 0.1 us)
Async XLA Ops:
  7.2 406.9 %copy-start = (bf16[1,384,4096]{2,1,0:T(8,128)(2,1)S(1)}, bf16[1,384,4096]{2,1,0:T(8,128)(2,1)}, u32[]{:S(2)}) copy-start(bf16[1,384,4096]{2,1,0:T(8,128)(2,1)} %param.27) | copy-start | bytes 9437188
  7.2 10.6 %copy-start.3 = (bf16[4096]{0:T(1024)(128)(2,1)S(1)}, bf16[4096]{0:T(1024)(128)(2,1)}, u32[]{:S(2)}) copy-start(bf16[4096]{0:T(1024)(128)(2,1)} %param.19) | copy-start | bytes 24580
  7.2 31.2 %all-gather.6.cloned.1.call-start = ((), (), s32[]{:S(2)}) async-start(), calls=%async_computation.3 | async-start | bytes 1310720 | tf_op jit(solution)/shard_map/all_gather | solution.py:79
  7.9 59.1 %all-gather.8.cloned.1.call-start = ((), (), s32[]{:S(2)}) async-start(), calls=%async_computation.4 | async-start | bytes 1310720 | tf_op jit(solution)/shard_map/all_gather | solution.py:80
  8.7 89.3 %all-gather.10.cloned.1.call-start = ((), (), s32[]{:S(2)}) async-start(), calls=%async_computation.5 | async-start | bytes 1310720 | tf_op jit(solution)/shard_map/all_gather | solution.py:77
  10.6 116.3 %all-gather.12.cloned.1.call-start = ((), (), s32[]{:S(2)}) async-start(), calls=%async_computation.6 | async-start | bytes 1310720 | tf_op jit(solution)/shard_map/all_gather | solution.py:78
  11.1 360.7 %all-gather.14.cloned.1.call-start = ((), (), s32[]{:S(2)}) async-start(), calls=%async_computation.7 | async-start | bytes 13107200 | tf_op jit(solution)/shard_map/all_gather | solution.py:99
  100.7 3.2 copy-start.1
  146.4 1.0 copy-start.2
  273.3 258.6 %reduce-scatter.2.cloned.1.call-start = ((), (), s32[]{:S(2)}) async-start(), calls=%async_computation.8 | async-start | bytes 13107200 | tf_op jit(solution)/shard_map/reduce_scatter | solution.py:107
  536.6 11.1 %copy-start.4 = (s32[128,2]{0,1:T(2,128)S(1)}, s32[128,2]{0,1:T(2,128)}, u32[]{:S(2)}) copy-start(s32[128,2]{0,1:T(2,128)} %param.24) | copy-start | bytes 3076
  536.6 107.3 %all-to-all-start.1 = ((bf16[64,5,4096]{2,1,0:T(8,128)(2,1)}), bf16[64,5,4096]{2,1,0:T(8,128)(2,1)}, u32[]{:S(2)}, u32[]{:S(2)}) async-start(bf16[64,5,4096]{2,1,0:T(8,128)(2,1)} %reshape.108), calls=%async_computation.2 | async-start | bytes 8388608 | tf_op jit(solution)/shard_map/all_to_all | solution.py:114
Sparse Core Ops, SparseCore 0:
  9.8 28.4 all-gather.5
  40.2 26.8 all-gather.7
  68.9 29.0 all-gather.9
  99.6 27.2 all-gather.11
  273.4 98.3 all-gather.13
  431.5 100.3 reduce-scatter.1
where the time goes:
time: 685 us; the launch traced here: 678 us
  waiting for transfers between devices  390 us (57%)
  blocking collectives  107 us (16%)
  local copies, waits for them, and re-layouts  89.1 us (13%)
  matrix products  47.2 us (7%)
  other arithmetic  18.4 us (3%)
  between operations  15.4 us (2%)
  starting transfers between devices  11.3 us (2%)
    all_to_all x1, blocking collectives, on_device(): lax.all_to_all(outgoing, 'ep', split_axis=0, concat_axis=0, tiled=True)  107 us
    reduce_scatter x1, waiting for transfers between devices, on_device(): lax.psum_scatter(jnp.dot(activated, down_local, preferred_element_type=jn...  101 us
    all_gather x1, waiting for transfers between devices, on_device(): arrived = lax.all_gather(received, 'sp', axis=0, tiled=True)  98.5 us
    all_to_all x1, waiting for transfers between devices, on_device(): lax.all_to_all(expert_out, 'ep', split_axis=0, concat_axis=0, tiled=True)  96 us
    all_gather x1, waiting for transfers between devices, on_device(): lax.all_gather(adapter_up, 'sp', axis=0, tiled=True)  28.7 us
    all_gather x1, waiting for transfers between devices, on_device(): lax.all_gather(key_heads, 'sp', axis=0, tiled=True)  23.3 us
    all_gather x1, waiting for transfers between devices, on_device(): lax.all_gather(adapter_down, 'sp', axis=0, tiled=True)  20.5 us
    all_gather x1, waiting for transfers between devices, on_device(): lax.all_gather(value_heads, 'sp', axis=0, tiled=True)  20.5 us
  transfers between devices with their start and end apart: 7, of which 7 were waited for; matrix products, arithmetic and copies ran while one was open for 3% of the time, Pallas kernels for 0%

commit v1 on v0

v1 whole, which is shorter than its diff:
```python
import functools

import jax
import jax.numpy as jnp
from jax import lax
from jax.experimental import pallas as pl
from jax.experimental.pallas import tpu as pltpu
from jax.sharding import PartitionSpec as P

D = 4096
HEADS = 32
KV_HEADS = 8
HEAD = 128
RANK = 32
SLOTS = 5
SEG = 8
WIDE = D // SEG
EXPERTS = 64
CHUNKS = (1, 2, 2)

epsilon = 1e-06
bf16 = jnp.bfloat16
f32 = jnp.float32
VMEM_SPEC = pl.BlockSpec(memory_space=pltpu.VMEM)
SMEM_SPEC = pl.BlockSpec(memory_space=pltpu.SMEM)
PARAMS = pltpu.CompilerParams(vmem_limit_bytes=56 << 20)


def dot(a, b, contract=((1,), (0,))):
    return lax.dot_general(a, b, (contract, ((), ())), preferred_element_type=f32)


def one_hot_dot(a, b, contract=((1,), (0,))):
    return dot(a, b, contract).astype(bf16)


def iota(shape, dim):
    return lax.broadcasted_iota(jnp.int32, shape, dim)


def to_segments():
    n = EXPERTS * SEG
    r, q = iota((n, n), 0), iota((n, n), 1)
    return (q == (r & (SEG - 1)) * EXPERTS + (r >> 3)).astype(f32).astype(bf16)


def from_segments():
    n = EXPERTS * SEG
    q, r = iota((n, n), 0), iota((n, n), 1)
    return (r == (q & (EXPERTS - 1)) * SEG + (q >> 6)).astype(f32).astype(bf16)


def slot_masks(routes_ref, start, tokens):
    own = routes_ref[:, pl.ds(start, tokens)]
    e = iota((EXPERTS, tokens), 0)
    first = (own[0:1, :] == e).astype(f32)
    second = (own[1:2, :] == e).astype(f32)
    before = (iota((tokens, tokens), 0) < iota((tokens, tokens), 1)).astype(f32)
    count = dot((first + second).astype(bf16), before.astype(bf16))
    return first, second, count


def attention_kernel(user_ref, sp_ref, stream, base, *refs):
    keys, values, adapters = refs[0:4], refs[4:8], refs[8:12]
    gain_a, gain_e, routes = refs[12:15]
    n_out = 1 + len(CHUNKS)
    hidden = refs[15]
    sends = refs[16 : 15 + n_out]
    xn, query, stack = refs[15 + n_out :]
    tokens = stream.shape[0]
    me = sp_ref[0]

    total = jnp.zeros((tokens, 1), f32)
    for s in range(SEG):
        x = stream[:, s * WIDE : (s + 1) * WIDE].astype(f32)
        total += jnp.sum(x * x, axis=1, keepdims=True)
    scale = lax.rsqrt(total * (1.0 / D) + epsilon)
    for s in range(SEG):
        cols = slice(s * WIDE, (s + 1) * WIDE)
        xn[:, cols] = (
            stream[:, cols].astype(f32) * scale * gain_a[:, cols].astype(f32)
        ).astype(bf16)

    quarter = D // 4
    starts = [
        pl.multiple_of(((me + shift) & 3) * quarter, quarter) for shift in (0, 3, 1, 2)
    ]
    low = jnp.zeros((tokens, RANK), f32)
    for start, part in zip(starts, adapters):
        low += dot(xn[:, pl.ds(start, quarter)], part[0:RANK, :], ((1,), (1,)))
    low = low.astype(bf16)
    for start, part in zip(starts, adapters):
        cols = pl.ds(start, quarter)
        delta = dot(low, part[RANK : 2 * RANK, :])
        query[:, cols] = (base[:, cols].astype(f32) + delta).astype(bf16)

    group = HEADS // KV_HEADS
    total = jnp.zeros((tokens, 1), f32)
    for g in range(KV_HEADS):
        kv = slice(g * HEAD, (g + 1) * HEAD)
        q = jnp.concatenate(
            [query[:, (g * group + h) * HEAD : (g * group + h + 1) * HEAD] for h in range(group)],
            axis=0,
        )
        k = jnp.concatenate([r[:, kv] for r in keys], axis=0)
        v = jnp.concatenate([r[:, kv] for r in values], axis=0)
        scores = dot(q, k, ((1,), (1,))) * HEAD ** (-0.5)
        e = jnp.exp(scores - jnp.max(scores, axis=1, keepdims=True))
        p = (e * (1.0 / jnp.sum(e, axis=1, keepdims=True))).astype(bf16)
        o = dot(p, v)
        for h in range(group):
            cols = slice((g * group + h) * HEAD, (g * group + h + 1) * HEAD)
            state = (
                stream[:, cols].astype(f32) + o[h * tokens : (h + 1) * tokens, :]
            ).astype(bf16)
            hidden[:, cols] = state
            wide = state.astype(f32)
            total += jnp.sum(wide * wide, axis=1, keepdims=True)

    scale = lax.rsqrt(total * (1.0 / D) + epsilon)
    first, second, count = slot_masks(routes, pl.multiple_of(me * tokens, tokens), tokens)
    named = first + second
    pick = jnp.concatenate(
        [jnp.where(count == c, named, 0.0) for c in range(SLOTS)], axis=0
    ).astype(bf16)
    for s in range(SEG):
        cols = slice(s * WIDE, (s + 1) * WIDE)
        hn = (hidden[:, cols].astype(f32) * scale * gain_e[:, cols].astype(f32)).astype(bf16)
        rows = one_hot_dot(pick, hn)
        for c in range(SLOTS):
            stack[s * EXPERTS : (s + 1) * EXPERTS, c * WIDE : (c + 1) * WIDE] = rows[
                c * EXPERTS : (c + 1) * EXPERTS, :
            ]
    order = to_segments()
    c = 0
    for n, send in zip(CHUNKS, sends):
        send[...] = one_hot_dot(order, stack[:, c * WIDE : (c + n) * WIDE])
        c += n


def attention(user, sp, stream, base, keys, values, adapters, gain_a, gain_e, routes):
    tokens = stream.shape[0]
    outs = [jax.ShapeDtypeStruct((tokens, D), bf16)] + [
        jax.ShapeDtypeStruct((EXPERTS * SEG, n * WIDE), bf16) for n in CHUNKS
    ]
    return pl.pallas_call(
        attention_kernel,
        out_shape=outs,
        in_specs=[SMEM_SPEC] * 2 + [VMEM_SPEC] * 17,
        out_specs=[VMEM_SPEC] * len(outs),
        scratch_shapes=[
            pltpu.VMEM((tokens, D), bf16),
            pltpu.VMEM((tokens, D), bf16),
            pltpu.VMEM((EXPERTS * SEG, SLOTS * WIDE), bf16),
        ],
        compiler_params=PARAMS,
        name="attention",
    )(user, sp, stream, base, *keys, *values, *adapters, gain_a, gain_e, routes)


def blocks_of(n):
    half = n * EXPERTS // 2
    for c in range(n):
        lo, hi = c * EXPERTS, (c + 1) * EXPERTS
        for which, (a, b) in enumerate(((0, half), (half, 2 * half))):
            x, y = max(lo, a), min(hi, b)
            if x < y:
                yield c, which, x - a, x - lo, y - x


def arrive_kernel(n, received, *halves):
    rows = one_hot_dot(from_segments(), received[...])
    for c, which, to, at, size in blocks_of(n):
        for s in range(SEG):
            halves[which][to : to + size, s * WIDE : (s + 1) * WIDE] = rows[
                s * EXPERTS + at : s * EXPERTS + at + size, c * WIDE : (c + 1) * WIDE
            ]


def arrive(n, received):
    half = jax.ShapeDtypeStruct((n * EXPERTS // 2, D), bf16)
    return pl.pallas_call(
        functools.partial(arrive_kernel, n),
        out_shape=[half, half],
        in_specs=[VMEM_SPEC],
        out_specs=[VMEM_SPEC] * 2,
        compiler_params=PARAMS,
        name="arrive",
    )(received)


def leave_kernel(n, *refs):
    terms, out, stack = (refs[0:3], refs[3:6]), refs[6], refs[7]
    for c, which, at, to, size in blocks_of(n):
        for s in range(SEG):
            cols = slice(s * WIDE, (s + 1) * WIDE)
            total = sum(t[at : at + size, cols].astype(f32) for t in terms[which])
            stack[
                s * EXPERTS + to : s * EXPERTS + to + size, c * WIDE : (c + 1) * WIDE
            ] = total.astype(bf16)
    out[...] = one_hot_dot(to_segments(), stack[...])


def leave(n, terms_a, terms_b):
    shape = (EXPERTS * SEG, n * WIDE)
    return pl.pallas_call(
        functools.partial(leave_kernel, n),
        out_shape=jax.ShapeDtypeStruct(shape, bf16),
        in_specs=[VMEM_SPEC] * 6,
        out_specs=VMEM_SPEC,
        scratch_shapes=[pltpu.VMEM(shape, bf16)],
        compiler_params=PARAMS,
        name="leave",
    )(*terms_a, *terms_b)


STEPS = 4


def expert_kernel(n, *refs):
    rows, (gate, up, down) = refs[0:n], refs[n : n + 3]
    outs = refs[n + 3 : 2 * n + 3]
    gate_sum, up_sum, act = refs[2 * n + 3 :]
    i = pl.program_id(0)
    depth = D // STEPS

    @pl.when(i == 0)
    def _():
        gate_sum[...] = jnp.zeros_like(gate_sum)
        up_sum[...] = jnp.zeros_like(up_sum)

    @pl.when(i < STEPS)
    def _():
        cols = pl.ds(pl.multiple_of(i * depth, depth), depth)
        x = jnp.concatenate([r[:, cols] for r in rows], axis=0)
        gate_sum[...] += dot(x, gate[...])
        up_sum[...] += dot(x, up[...])

    @pl.when(i == STEPS - 1)
    def _():
        v = gate_sum[...]
        act[...] = (v / (1.0 + jnp.exp(-v)) * up_sum[...]).astype(bf16)

    @pl.when(i >= STEPS)
    def _():
        part = dot(act[...], down[...]).astype(bf16)
        size = rows[0].shape[0]
        for k in range(n):
            outs[k][...] = part[k * size : (k + 1) * size, :]


def expert(pieces, gate, up, down):
    n, size, hidden = len(pieces), pieces[0].shape[0], gate.shape[1]
    depth = D // STEPS
    first = lambda i: (jnp.minimum(i, STEPS - 1), 0)
    last = lambda i: (0, jnp.maximum(i - STEPS, 0))
    flops = 6 * n * size * D * hidden
    return pl.pallas_call(
        functools.partial(expert_kernel, n),
        out_shape=[jax.ShapeDtypeStruct((size, D), bf16)] * n,
        grid=(2 * STEPS,),
        in_specs=[pl.BlockSpec((size, D), lambda i: (0, 0))] * n
        + [pl.BlockSpec((depth, hidden), first)] * 2
        + [pl.BlockSpec((hidden, depth), last)],
        out_specs=[pl.BlockSpec((size, depth), last)] * n,
        scratch_shapes=[
            pltpu.VMEM((n * size, hidden), f32),
            pltpu.VMEM((n * size, hidden), f32),
            pltpu.VMEM((n * size, hidden), bf16),
        ],
        compiler_params=PARAMS,
        cost_estimate=pl.CostEstimate(
            flops=flops,
            transcendentals=n * size * hidden,
            bytes_accessed=6 * D * hidden + 4 * n * size * D,
        ),
        name="expert",
    )(*pieces, gate, up, down)


def combine_kernel(sp_ref, routes, weights, *refs):
    received, out, stack = refs[: len(CHUNKS)], refs[-2], refs[-1]
    tokens = out.shape[0]
    first, second, count = slot_masks(routes, pl.multiple_of(sp_ref[0] * tokens, tokens), tokens)
    w = weights[...].astype(f32)
    w = w / jnp.sum(w, axis=0, keepdims=True)
    share = first * w[0:1, :] + second * w[1:2, :]
    share = jnp.concatenate(
        [jnp.where(count == c, share, 0.0) for c in range(SLOTS)], axis=0
    )
    high = share.astype(bf16)
    rest = (share - high.astype(f32)).astype(bf16)
    order = from_segments()
    c = 0
    for n, r in zip(CHUNKS, received):
        stack[:, c * WIDE : (c + n) * WIDE] = one_hot_dot(order, r[...])
        c += n
    for s in range(SEG):
        rows = jnp.concatenate(
            [
                stack[s * EXPERTS : (s + 1) * EXPERTS, k * WIDE : (k + 1) * WIDE]
                for k in range(SLOTS)
            ],
            axis=0,
        )
        both = dot(high, rows, ((0,), (0,))) + dot(rest, rows, ((0,), (0,)))
        out[:, s * WIDE : (s + 1) * WIDE] = both.astype(bf16)


def combine(sp, routes, weights, received, tokens):
    return pl.pallas_call(
        combine_kernel,
        out_shape=jax.ShapeDtypeStruct((tokens, D), bf16),
        in_specs=[SMEM_SPEC] + [VMEM_SPEC] * (2 + len(received)),
        out_specs=VMEM_SPEC,
        scratch_shapes=[pltpu.VMEM((EXPERTS * SEG, SLOTS * WIDE), bf16)],
        compiler_params=PARAMS,
        name="combine",
    )(sp, routes, weights, *received)


def right(x):
    return lax.ppermute(x, "sp", [(i, (i + 1) % 4) for i in range(4)])


def left(x):
    return lax.ppermute(x, "sp", [(i, (i + 3) % 4) for i in range(4)])


def exchange(x, n):
    cut = x.reshape(EXPERTS, SEG, n * WIDE)
    moved = lax.all_to_all(cut, "ep", split_axis=0, concat_axis=0, tiled=True)
    return moved.reshape(EXPERTS * SEG, n * WIDE)


def feed_forward(n, sent, gate, up, down):
    a, b = arrive(n, exchange(sent, n))
    a_left, a_right = right(a), left(a)
    b_left, b_right = right(b), left(b)
    a_far, b_far = right(a_left), left(b_right)
    pa_far, pb_far = expert([a_far, b_far], gate, up, down)
    a_in, b_in = right(pa_far), left(pb_far)
    pa_left, pb_left, pa_right, pb_right = expert(
        [a_left, b_left, a_right, b_right], gate, up, down
    )
    pa, pb = expert([a, b], gate, up, down)
    add = lambda x, y: (x.astype(f32) + y.astype(f32)).astype(bf16)
    a_from_left, b_from_left = right(add(pa_right, a_in)), right(pb_right)
    a_from_right, b_from_right = left(pa_left), left(add(pb_left, b_in))
    out = leave(n, (pa, a_from_left, a_from_right), (pb, b_from_left, b_from_right))
    return exchange(out, n)


def on_device(
    stream,
    query_base,
    key_heads,
    value_heads,
    attention_gain,
    expert_gain,
    adapter_down,
    adapter_up,
    user_index,
    routes,
    route_weights,
    gate_weight,
    up_weight,
    down_weight,
):
    sp = lax.axis_index("sp").astype(jnp.int32).reshape(1)
    columns = user_index[0] * RANK + jnp.arange(RANK, dtype=jnp.int32)
    select = (columns[:, None] == jnp.arange(4 * RANK, dtype=jnp.int32)[None, :]).astype(bf16)
    adapter = jnp.concatenate(
        [
            one_hot_dot(select, adapter_down, ((1,), (1,))),
            one_hot_dot(select, adapter_up, ((1,), (1,))),
        ],
        axis=0,
    )
    k_left, k_right = right(key_heads), left(key_heads)
    v_left, v_right = right(value_heads), left(value_heads)
    d_left, d_right = right(adapter), left(adapter)
    keys = (key_heads, k_left, k_right, right(k_left))
    values = (value_heads, v_left, v_right, left(v_right))
    adapters = (adapter, d_left, d_right, right(d_left))
    routes_t, weights_t = routes.T, route_weights.T
    hidden, *sends = attention(
        user_index,
        sp,
        stream,
        query_base,
        keys,
        values,
        adapters,
        attention_gain.reshape(1, D),
        expert_gain.reshape(1, D),
        routes_t,
    )
    gate, up, down = gate_weight[0], up_weight[0], down_weight[0]
    received = [feed_forward(n, x, gate, up, down) for n, x in zip(CHUNKS, sends)]
    moe_out = combine(sp, routes_t, weights_t, received, stream.shape[0])
    return (hidden, moe_out)


def solution(mesh):
    in_specs = (
        P(("ep", "sp"), None),
        P(("ep", "sp"), None),
        P(("ep", "sp"), None),
        P(("ep", "sp"), None),
        P(),
        P(),
        P("sp", None),
        P("sp", None),
        P("ep"),
        P("ep", None),
        P(("ep", "sp"), None),
        P("ep", None, "sp"),
        P("ep", None, "sp"),
        P("ep", "sp", None),
    )
    out_specs = (P(("ep", "sp"), None), P(("ep", "sp"), None))
    return jax.shard_map(
        on_device, mesh=mesh, in_specs=in_specs, out_specs=out_specs, check_vma=False
    )
```

time: 685 us -> 382 us (0.56)
  the two profiles are of different devices: /device:TPU:6 before, /device:TPU:4 now
where the time goes in v1:
time: 382 us; the launch traced here: 375 us
  Pallas kernels  119 us (31%)
  starting transfers between devices  92.5 us (24%)
  waiting for transfers between devices  82.2 us (22%)
  blocking collectives  64.4 us (17%)
  local copies, waits for them, and re-layouts  7.99 us (2%)
  other arithmetic  5.67 us (1%)
    pallas_call x9, Pallas kernels, expert(): pl.pallas_call(functools.partial(expert_kernel, n), out_shape=[jax.ShapeD...  83.5 us
    all_to_all x2, blocking collectives, exchange(): moved = lax.all_to_all(cut, 'ep', split_axis=0, concat_axis=0, tiled=True)  64.4 us
    ppermute x23, waiting for transfers between devices, right(): return lax.ppermute(x, 'sp', [(i, (i + 1) % 4) for i in range(4)])  53.7 us
    ppermute x23, starting transfers between devices, right(): return lax.ppermute(x, 'sp', [(i, (i + 1) % 4) for i in range(4)])  42.1 us
    all_to_all x4, starting transfers between devices, exchange(): moved = lax.all_to_all(cut, 'ep', split_axis=0, concat_axis=0, tiled=True)  32.1 us
    all_to_all x4, waiting for transfers between devices, exchange(): moved = lax.all_to_all(cut, 'ep', split_axis=0, concat_axis=0, tiled=True)  24.3 us
    ppermute x22, starting transfers between devices, left(): return lax.ppermute(x, 'sp', [(i, (i + 3) % 4) for i in range(4)])  18.3 us
    pallas_call x1, Pallas kernels, attention(): pl.pallas_call(attention_kernel, out_shape=outs, in_specs=[SMEM_SPEC] * 2...  12 us
  transfers between devices with their start and end apart: 49, of which 13 were waited for; matrix products, arithmetic and copies ran while one was open for 3% of the time, Pallas kernels for 27%

profile of v1, /device:TPU:4, one launch (start us, length us, event | category | flops | bytes accessed | tf_op | source)
XLA Modules:
  0.0 375.1 jit_solution(5751129092891741137)
XLA Ops:
  0.6 1.3 collective-permute-start
  4.9 1.5 collective-permute-start.6
  7.0 2.1 collective-permute-start.1
  9.1 2.7 collective-permute-done.6.refs_9_
  11.8 1.2 collective-permute-start.3
  13.0 2.8 collective-permute-start.2
  15.8 2.2 collective-permute-start.8
  18.0 1.3 reshape.56.refs_12_
  19.3 1.3 reshape.57.refs_13_
  20.6 7.0 %collective-permute-done.8.refs_11_ = bf16[64,1024]{1,0:T(8,128)(2,1)S(1)} collective-permute-done((bf16[64,1024]{1,0:T(8,128)(2,1)S(1)}, bf16[64,1024]{1,0:T(8,128)(2,1)S(1)}, u32[]{:S(2)}, u32[]{:S(2)}) %collective-permute-start.8) | collective-permute-done | bytes 131104 | tf_op jit(solution)/shard_map/ppermute | solution.py:323
  28.6 12.0 %attention.1 = (bf16[128,4096]{1,0:T(8,128)(2,1)}, bf16[512,512]{1,0:T(8,128)(2,1)}, bf16[512,1024]{1,0:T(8,128)(2,1)}, bf16[512,1024]{1,0:T(8,128)(2,1)}) custom-call(s32[1]{0:T(128)S(6)} %copy.16.user_ref, s32[1]{0:T(128)} %bitcast.sp_ref, bf16[128,4096]{1,0:T(8,128)(2,1)} %stream.1, bf16[128,4096]{1,0:T(8,128)(2,1)} %base.1, bf16[128,1024]{1,0:T(8,128)(2,1)} %refs_0_.1, ...), custom_call_target="tpu_custom_call" | custom-call | tf_op jit(solution)/shard_map/attention/pallas_call | solution.py:146
  40.6 29.9 %all_to_all.30 = bf16[64,8,512]{2,1,0:T(8,128)(2,1)} all-to-all(bf16[64,8,512]{2,1,0:T(8,128)(2,1)} %bitcast.58), channel_id=1, replica_groups=mesh['ep'=64,'sp'=4] {'ep'}, dimensions={0} | all-to-all | bytes 1048576 | tf_op jit(solution)/shard_map/all_to_all | solution.py:332
  70.5 5.8 %all-to-all-start.4 = ((bf16[64,8,1024]{2,1,0:T(8,128)(2,1)}), bf16[64,8,1024]{2,1,0:T(8,128)(2,1)S(1)}, u32[]{:S(2)}, u32[]{:S(2)}) async-start(bf16[64,8,1024]{2,1,0:T(8,128)(2,1)} %bitcast.57), calls=%async_computation.4 | async-start | bytes 2097152 | tf_op jit(solution)/shard_map/all_to_all | solution.py:332
  76.3 2.3 arrive.3
  78.5 1.2 collective-permute-start.9
  80.6 6.4 %collective-permute-done.9.refs_0_ = bf16[32,4096]{1,0:T(8,128)(2,1)S(1)} collective-permute-done((bf16[32,4096]{1,0:T(8,128)(2,1)}, bf16[32,4096]{1,0:T(8,128)(2,1)S(1)}, u32[]{:S(2)}, u32[]{:S(2)}) %collective-permute-start.9) | collective-permute-done | bytes 262176 | tf_op jit(solution)/shard_map/ppermute | solution.py:323
  87.0 2.4 collective-permute-start.13
  89.6 15.6 %all-to-all-done.4 = bf16[64,8,1024]{2,1,0:T(8,128)(2,1)S(1)} async-done(((bf16[64,8,1024]{2,1,0:T(8,128)(2,1)}), bf16[64,8,1024]{2,1,0:T(8,128)(2,1)S(1)}, u32[]{:S(2)}, u32[]{:S(2)}) %all-to-all-start.4) | async-done | bytes 1048608 | tf_op jit(solution)/shard_map/all_to_all | solution.py:332
  106.1 2.7 arrive.5
  108.9 1.2 collective-permute-start.33
  110.9 2.4 collective-permute-start.10
  114.1 8.4 %expert.11 = (bf16[32,4096]{1,0:T(8,128)(2,1)}, bf16[32,4096]{1,0:T(8,128)(2,1)}) custom-call(bf16[32,4096]{1,0:T(8,128)(2,1)} %copy-done.36, bf16[32,4096]{1,0:T(8,128)(2,1)} %copy-done.37, bf16[4096,384]{1,0:T(8,128)(2,1)} %bitcast.21, bf16[4096,384]{1,0:T(8,128)(2,1)} %bitcast.30, bf16[384,4096]{1,0:T(8,128)(2,1)} %bitcast.39), custom_call_target="tpu_custom_call" | custom-call | flops 603979776 | bytes 10485760 | tf_op jit(solution)/shard_map/expert/pallas_call | solution.py:258
  122.5 2.6 collective-permute-start.19
  125.1 5.6 %all-to-all-start.2 = ((bf16[64,8,1024]{2,1,0:T(8,128)(2,1)}), bf16[64,8,1024]{2,1,0:T(8,128)(2,1)S(1)}, u32[]{:S(2)}, u32[]{:S(2)}) async-start(bf16[64,8,1024]{2,1,0:T(8,128)(2,1)} %bitcast.11), calls=%async_computation.2 | async-start | bytes 2097152 | tf_op jit(solution)/shard_map/all_to_all | solution.py:332
  130.7 1.3 collective-permute-done.11.refs_2_
  132.0 9.0 %expert.10 = (bf16[32,4096]{1,0:T(8,128)(2,1)}, bf16[32,4096]{1,0:T(8,128)(2,1)}, bf16[32,4096]{1,0:T(8,128)(2,1)}, bf16[32,4096]{1,0:T(8,128)(2,1)}) custom-call(bf16[32,4096]{1,0:T(8,128)(2,1)} %copy-done.29, bf16[32,4096]{1,0:T(8,128)(2,1)} %collective-permute-done.10.refs_1_, bf16[32,4096]{1,0:T(8,128)(2,1)} %collective-permute-done.11.refs_2_, ...), custom_call_target="tpu_custom_call" | custom-call | flops 1207959552 | bytes 11534336 | tf_op jit(solution)/shard_map/expert/pallas_call | solution.py:258
  141.1 1.9 collective-permute-start.17
  143.0 1.4 collective-permute-start.18
  144.4 3.1 collective-permute-start.15
  147.7 1.9 collective-permute-start.38
  149.6 1.8 add_convert_fusion.4
  151.4 16.6 %collective-permute-done.37.refs_0_ = bf16[64,4096]{1,0:T(8,128)(2,1)S(1)} collective-permute-done((bf16[64,4096]{1,0:T(8,128)(2,1)S(1)}, bf16[64,4096]{1,0:T(8,128)(2,1)S(1)}, u32[]{:S(2)}, u32[]{:S(2)}) %collective-permute-start.37) | collective-permute-done | bytes 524320 | tf_op jit(solution)/shard_map/ppermute | solution.py:323
  168.4 1.9 collective-permute-start.34
  170.3 9.0 %expert.17 = (bf16[64,4096]{1,0:T(8,128)(2,1)}, bf16[64,4096]{1,0:T(8,128)(2,1)}) custom-call(bf16[64,4096]{1,0:T(8,128)(2,1)} %copy-done.18, bf16[64,4096]{1,0:T(8,128)(2,1)} %copy-done.19, bf16[4096,384]{1,0:T(8,128)(2,1)} %bitcast.23, bf16[4096,384]{1,0:T(8,128)(2,1)} %bitcast.32, bf16[384,4096]{1,0:T(8,128)(2,1)} %bitcast.41), custom_call_target="tpu_custom_call" | custom-call | flops 1207959552 | bytes 11534336 | tf_op jit(solution)/shard_map/expert/pallas_call | solution.py:258
  179.8 1.3 collective-permute-start.43
  182.0 8.4 %expert.9 = (bf16[32,4096]{1,0:T(8,128)(2,1)}, bf16[32,4096]{1,0:T(8,128)(2,1)}) custom-call(bf16[32,4096]{1,0:T(8,128)(2,1)} %get-tuple-element.38.refs_0_, bf16[32,4096]{1,0:T(8,128)(2,1)} %get-tuple-element.39.refs_1_, bf16[4096,384]{1,0:T(8,128)(2,1)} %bitcast.24, bf16[4096,384]{1,0:T(8,128)(2,1)} %bitcast.33, bf16[384,4096]{1,0:T(8,128)(2,1)} %bitcast.42), custom_call_target="tpu_custom_call" | custom-call | flops 603979776 | bytes 10485760 | tf_op jit(solution)/shard_map/expert/pallas_call | solution.py:258
  191.4 2.7 arrive.4
  194.2 2.4 collective-permute-start.24
  197.1 2.7 leave.3
  199.8 10.4 %all-to-all-start.1 = ((bf16[64,8,512]{2,1,0:T(8,128)(2,1)}), bf16[64,8,512]{2,1,0:T(8,128)(2,1)S(1)}, u32[]{:S(2)}, u32[]{:S(2)}) async-start(bf16[64,8,512]{2,1,0:T(8,128)(2,1)} %bitcast.56), calls=%async_computation.1 | async-start | bytes 1048576 | tf_op jit(solution)/shard_map/all_to_all | solution.py:332
  210.2 3.2 collective-permute-start.21
  213.5 10.8 %expert.16 = (bf16[64,4096]{1,0:T(8,128)(2,1)}, bf16[64,4096]{1,0:T(8,128)(2,1)}, bf16[64,4096]{1,0:T(8,128)(2,1)}, bf16[64,4096]{1,0:T(8,128)(2,1)}) custom-call(bf16[64,4096]{1,0:T(8,128)(2,1)} %copy-done.8, bf16[64,4096]{1,0:T(8,128)(2,1)} %collective-permute-done.34.refs_1_, bf16[64,4096]{1,0:T(8,128)(2,1)} %collective-permute-done.35.refs_2_, ...), custom_call_target="tpu_custom_call" | custom-call | flops 2415919104 | bytes 13631488 | tf_op jit(solution)/shard_map/expert/pallas_call | solution.py:258
  224.3 2.1 collective-permute-start.39
  226.3 1.3 add_convert_fusion
  227.8 2.2 collective-permute-start.25
  230.0 9.2 %collective-permute-done.39 = bf16[64,4096]{1,0:T(8,128)(2,1)S(1)} collective-permute-done((bf16[64,4096]{1,0:T(8,128)(2,1)S(1)}, bf16[64,4096]{1,0:T(8,128)(2,1)S(1)}, u32[]{:S(2)}, u32[]{:S(2)}) %collective-permute-start.39) | collective-permute-done | bytes 524320 | tf_op jit(solution)/shard_map/ppermute | solution.py:323
  241.2 1.3 collective-permute-start.42
  242.5 7.9 %collective-permute-done.25.refs_0_ = bf16[64,4096]{1,0:T(8,128)(2,1)S(1)} collective-permute-done((bf16[64,4096]{1,0:T(8,128)(2,1)S(1)}, bf16[64,4096]{1,0:T(8,128)(2,1)S(1)}, u32[]{:S(2)}, u32[]{:S(2)}) %collective-permute-start.25) | collective-permute-done | bytes 524320 | tf_op jit(solution)/shard_map/ppermute | solution.py:323
  251.3 2.5 collective-permute-done.26.refs_1_
  253.8 2.9 collective-permute-start.40
  256.7 9.0 %expert.14 = (bf16[64,4096]{1,0:T(8,128)(2,1)}, bf16[64,4096]{1,0:T(8,128)(2,1)}) custom-call(bf16[64,4096]{1,0:T(8,128)(2,1)} %copy-done.16, bf16[64,4096]{1,0:T(8,128)(2,1)} %copy-done.17, bf16[4096,384]{1,0:T(8,128)(2,1)} %bitcast.26, bf16[4096,384]{1,0:T(8,128)(2,1)} %bitcast.35, bf16[384,4096]{1,0:T(8,128)(2,1)} %bitcast.44), custom_call_target="tpu_custom_call" | custom-call | flops 1207959552 | bytes 11534336 | tf_op jit(solution)/shard_map/expert/pallas_call | solution.py:258
  265.9 9.1 %expert.15 = (bf16[64,4096]{1,0:T(8,128)(2,1)}, bf16[64,4096]{1,0:T(8,128)(2,1)}) custom-call(bf16[64,4096]{1,0:T(8,128)(2,1)} %get-tuple-element.60.refs_0_, bf16[64,4096]{1,0:T(8,128)(2,1)} %get-tuple-element.61.refs_1_, bf16[4096,384]{1,0:T(8,128)(2,1)} %bitcast.27, bf16[4096,384]{1,0:T(8,128)(2,1)} %bitcast.36, bf16[384,4096]{1,0:T(8,128)(2,1)} %bitcast.45), custom_call_target="tpu_custom_call" | custom-call | flops 1207959552 | bytes 11534336 | tf_op jit(solution)/shard_map/expert/pallas_call | solution.py:258
  275.0 10.7 %expert.13 = (bf16[64,4096]{1,0:T(8,128)(2,1)}, bf16[64,4096]{1,0:T(8,128)(2,1)}, bf16[64,4096]{1,0:T(8,128)(2,1)}, bf16[64,4096]{1,0:T(8,128)(2,1)}) custom-call(bf16[64,4096]{1,0:T(8,128)(2,1)} %copy-done.12, bf16[64,4096]{1,0:T(8,128)(2,1)} %copy-done.11, bf16[64,4096]{1,0:T(8,128)(2,1)} %copy-done.13, bf16[64,4096]{1,0:T(8,128)(2,1)} %copy-done.10, ...), custom_call_target="tpu_custom_call" | custom-call | flops 2415919104 | bytes 13631488 | tf_op jit(solution)/shard_map/expert/pallas_call | solution.py:258
  285.8 2.0 collective-permute-start.30
  287.8 3.1 collective-permute-start.27
  291.8 3.8 %leave.5 = bf16[512,1024]{1,0:T(8,128)(2,1)} custom-call(bf16[64,4096]{1,0:T(8,128)(2,1)} %get-tuple-element.62.refs_0_, bf16[64,4096]{1,0:T(8,128)(2,1)} %copy-done.24, bf16[64,4096]{1,0:T(8,128)(2,1)} %copy-done.21, bf16[64,4096]{1,0:T(8,128)(2,1)} %get-tuple-element.66.refs_3_, bf16[64,4096]{1,0:T(8,128)(2,1)} %copy-done.22, bf16[64,4096]{1,0:T(8,128)(2,1)} %copy-done.23), custom_call_target="tpu_custom_call" | custom-call | tf_op jit(solution)/shard_map/leave/pallas_call | solution.py:206
  295.5 10.4 %all-to-all-start.5 = ((bf16[64,8,1024]{2,1,0:T(8,128)(2,1)}), bf16[64,8,1024]{2,1,0:T(8,128)(2,1)S(1)}, u32[]{:S(2)}, u32[]{:S(2)}) async-start(bf16[64,8,1024]{2,1,0:T(8,128)(2,1)} %bitcast.52), calls=%async_computation.5 | async-start | bytes 2097152 | tf_op jit(solution)/shard_map/all_to_all | solution.py:332
  306.1 2.2 collective-permute-done.27
  310.7 9.0 %expert.12 = (bf16[64,4096]{1,0:T(8,128)(2,1)}, bf16[64,4096]{1,0:T(8,128)(2,1)}) custom-call(bf16[64,4096]{1,0:T(8,128)(2,1)} %get-tuple-element.49.refs_0_, bf16[64,4096]{1,0:T(8,128)(2,1)} %get-tuple-element.50.refs_1_, bf16[4096,384]{1,0:T(8,128)(2,1)} %bitcast.29, bf16[4096,384]{1,0:T(8,128)(2,1)} %bitcast.38, bf16[384,4096]{1,0:T(8,128)(2,1)} %bitcast.47), custom_call_target="tpu_custom_call" | custom-call | flops 1207959552 | bytes 11534336 | tf_op jit(solution)/shard_map/expert/pallas_call | solution.py:258
  320.0 1.5 collective-permute-done.28.refs_1_
  322.4 3.7 leave.4
  326.0 8.8 %all-to-all-done.5 = bf16[64,8,1024]{2,1,0:T(8,128)(2,1)S(1)} async-done(((bf16[64,8,1024]{2,1,0:T(8,128)(2,1)}), bf16[64,8,1024]{2,1,0:T(8,128)(2,1)S(1)}, u32[]{:S(2)}, u32[]{:S(2)}) %all-to-all-start.5) | async-done | bytes 1048608 | tf_op jit(solution)/shard_map/all_to_all | solution.py:332
  334.8 34.6 %all_to_all.31 = bf16[64,8,1024]{2,1,0:T(8,128)(2,1)} all-to-all(bf16[64,8,1024]{2,1,0:T(8,128)(2,1)} %bitcast.53), channel_id=1, replica_groups=mesh['ep'=64,'sp'=4] {'ep'}, dimensions={0} | all-to-all | bytes 2097152 | tf_op jit(solution)/shard_map/all_to_all | solution.py:332
  369.3 5.3 %combine.1 = bf16[128,4096]{1,0:T(8,128)(2,1)} custom-call(s32[1]{0:T(128)} %bitcast.sp_ref, s32[2,512]{1,0:T(2,128)} %bitcast.60, s32[2,128]{1,0:T(2,128)} %bitcast.61, bf16[512,512]{1,0:T(8,128)(2,1)} %bitcast.54, bf16[512,1024]{1,0:T(8,128)(2,1)} %bitcast.49, bf16[512,1024]{1,0:T(8,128)(2,1)} %bitcast.48), custom_call_target="tpu_custom_call" | custom-call | tf_op jit(solution)/shard_map/combine/pallas_call | solution.py:311
  (157 shorter events, 18.5 us)
Async XLA Ops:
  0.6 12.3 %collective-permute-start = (bf16[128,1024]{1,0:T(8,128)(2,1)}, bf16[128,1024]{1,0:T(8,128)(2,1)S(1)}, u32[]{:S(2)}, u32[]{:S(2)}) collective-permute-start(bf16[128,1024]{1,0:T(8,128)(2,1)} %refs_0_.1), channel_id=1, source_target_pairs={{0,1},{1,2},{2,3},{3,0},{4,5},{5,6},{6,7},{7,4},{8,9},{9,10},{10,1... | collective-permute-start | bytes 786440 | tf_op jit(solution)/shard_map/ppermute | solution.py:323
  1.9 13.8 %collective-permute-start.4 = (bf16[128,1024]{1,0:T(8,128)(2,1)}, bf16[128,1024]{1,0:T(8,128)(2,1)S(1)}, u32[]{:S(2)}, u32[]{:S(2)}) collective-permute-start(bf16[128,1024]{1,0:T(8,128)(2,1)} %refs_4_.1), channel_id=1, source_target_pairs={{0,3},{1,0},{2,1},{3,2},{4,7},{5,4},{6,5},{7,6},{8,11},{9,8},{10,9... | collective-permute-start | bytes 786440 | tf_op jit(solution)/shard_map/ppermute | solution.py:327
  4.9 22.8 %copy-start.20 = (bf16[64,1024]{1,0:T(8,128)(2,1)}, bf16[64,1024]{1,0:T(8,128)(2,1)S(1)}, u32[]{:S(2)}) copy-start(bf16[64,1024]{1,0:T(8,128)(2,1)S(1)} %pad_maximum_fusion.refs_8_) | copy-start | bytes 393220
  4.9 6.9 %collective-permute-start.6 = (bf16[64,1024]{1,0:T(8,128)(2,1)S(1)}, bf16[64,1024]{1,0:T(8,128)(2,1)S(1)}, u32[]{:S(2)}, u32[]{:S(2)}) collective-permute-start(bf16[64,1024]{1,0:T(8,128)(2,1)S(1)} %pad_maximum_fusion.refs_8_), channel_id=1, source_target_pairs={{0,1},{1,2},{2,3},{3,0},{4,5},{5,6},{6,7},{7,4},{8,9},{9,10},{10,1... | collective-permute-start | bytes 393224 | tf_op jit(solution)/shard_map/ppermute | solution.py:323
  6.3 9.4 %collective-permute-start.7 = (bf16[64,1024]{1,0:T(8,128)(2,1)S(1)}, bf16[64,1024]{1,0:T(8,128)(2,1)S(1)}, u32[]{:S(2)}, u32[]{:S(2)}) collective-permute-start(bf16[64,1024]{1,0:T(8,128)(2,1)S(1)} %pad_maximum_fusion.refs_8_), channel_id=1, source_target_pairs={{0,3},{1,0},{2,1},{3,2},{4,7},{5,4},{6,5},{7,6},{8,11},{9,8},{10,9... | collective-permute-start | bytes 393224 | tf_op jit(solution)/shard_map/ppermute | solution.py:327
  7.0 20.6 %collective-permute-start.1 = (bf16[128,1024]{1,0:T(8,128)(2,1)}, bf16[128,1024]{1,0:T(8,128)(2,1)S(1)}, u32[]{:S(2)}, u32[]{:S(2)}) collective-permute-start(bf16[128,1024]{1,0:T(8,128)(2,1)} %refs_0_.1), channel_id=1, source_target_pairs={{0,3},{1,0},{2,1},{3,2},{4,7},{5,4},{6,5},{7,6},{8,11},{9,8},{10,9... | collective-permute-start | bytes 786440 | tf_op jit(solution)/shard_map/ppermute | solution.py:327
  11.8 15.8 %collective-permute-start.3 = (bf16[128,1024]{1,0:T(8,128)(2,1)}, bf16[128,1024]{1,0:T(8,128)(2,1)S(1)}, u32[]{:S(2)}, u32[]{:S(2)}) collective-permute-start(bf16[128,1024]{1,0:T(8,128)(2,1)} %refs_4_.1), channel_id=1, source_target_pairs={{0,1},{1,2},{2,3},{3,0},{4,5},{5,6},{6,7},{7,4},{8,9},{9,10},{10,1... | collective-permute-start | bytes 786440 | tf_op jit(solution)/shard_map/ppermute | solution.py:323
  13.0 14.6 %collective-permute-start.2 = (bf16[128,1024]{1,0:T(8,128)(2,1)S(1)}, bf16[128,1024]{1,0:T(8,128)(2,1)S(1)}, u32[]{:S(2)}, u32[]{:S(2)}) collective-permute-start(bf16[128,1024]{1,0:T(8,128)(2,1)S(1)} %collective-permute-done.refs_1_), channel_id=1, source_target_pairs={{0,1},{1,2},{2,3},{3,0},{4,5},{5,6},{6,7},{7,4},{8,9},{9,10},{10,1... | collective-permute-start | bytes 786440 | tf_op jit(solution)/shard_map/ppermute | solution.py:323
  15.8 11.9 %collective-permute-start.5 = (bf16[128,1024]{1,0:T(8,128)(2,1)S(1)}, bf16[128,1024]{1,0:T(8,128)(2,1)S(1)}, u32[]{:S(2)}, u32[]{:S(2)}) collective-permute-start(bf16[128,1024]{1,0:T(8,128)(2,1)S(1)} %collective-permute-done.4.refs_6_), channel_id=1, source_target_pairs={{0,3},{1,0},{2,1},{3,2},{4,7},{5,4},{6,5},{7,6},{8,11},{9,8},{10,9... | collective-permute-start | bytes 786440 | tf_op jit(solution)/shard_map/ppermute | solution.py:327
  15.8 11.8 %collective-permute-start.8 = (bf16[64,1024]{1,0:T(8,128)(2,1)S(1)}, bf16[64,1024]{1,0:T(8,128)(2,1)S(1)}, u32[]{:S(2)}, u32[]{:S(2)}) collective-permute-start(bf16[64,1024]{1,0:T(8,128)(2,1)S(1)} %collective-permute-done.6.refs_9_), channel_id=1, source_target_pairs={{0,1},{1,2},{2,3},{3,0},{4,5},{5,6},{6,7},{7,4},{8,9},{9,10},{10,1... | collective-permute-start | bytes 393224 | tf_op jit(solution)/shard_map/ppermute | solution.py:323
  70.5 34.7 %all-to-all-start.4 = ((bf16[64,8,1024]{2,1,0:T(8,128)(2,1)}), bf16[64,8,1024]{2,1,0:T(8,128)(2,1)S(1)}, u32[]{:S(2)}, u32[]{:S(2)}) async-start(bf16[64,8,1024]{2,1,0:T(8,128)(2,1)} %bitcast.57), calls=%async_computation.4 | async-start | bytes 2097152 | tf_op jit(solution)/shard_map/all_to_all | solution.py:332
  78.5 8.5 %collective-permute-start.9 = (bf16[32,4096]{1,0:T(8,128)(2,1)}, bf16[32,4096]{1,0:T(8,128)(2,1)S(1)}, u32[]{:S(2)}, u32[]{:S(2)}) collective-permute-start(bf16[32,4096]{1,0:T(8,128)(2,1)} %get-tuple-element.38.refs_0_), channel_id=1, source_target_pairs={{0,1},{1,2},{2,3},{3,0},{4,5},{5,6},{6,7},{7,4},{8,9},{9,10},{10,1... | collective-permute-start | bytes 786440 | tf_op jit(solution)/shard_map/ppermute | solution.py:323
  79.7 9.7 %collective-permute-start.12 = (bf16[32,4096]{1,0:T(8,128)(2,1)}, bf16[32,4096]{1,0:T(8,128)(2,1)S(1)}, u32[]{:S(2)}, u32[]{:S(2)}) collective-permute-start(bf16[32,4096]{1,0:T(8,128)(2,1)} %get-tuple-element.39.refs_1_), channel_id=1, source_target_pairs={{0,3},{1,0},{2,1},{3,2},{4,7},{5,4},{6,5},{7,6},{8,11},{9,8},{10,9... | collective-permute-start | bytes 786440 | tf_op jit(solution)/shard_map/ppermute | solution.py:327
  87.0 45.0 %copy-start.29 = (bf16[32,4096]{1,0:T(8,128)(2,1)}, bf16[32,4096]{1,0:T(8,128)(2,1)S(1)}, u32[]{:S(2)}) copy-start(bf16[32,4096]{1,0:T(8,128)(2,1)S(1)} %collective-permute-done.9.refs_0_) | copy-start | bytes 786436
  87.0 26.3 %collective-permute-start.13 = (bf16[32,4096]{1,0:T(8,128)(2,1)S(1)}, bf16[32,4096]{1,0:T(8,128)(2,1)S(1)}, u32[]{:S(2)}, u32[]{:S(2)}) collective-permute-start(bf16[32,4096]{1,0:T(8,128)(2,1)S(1)} %collective-permute-done.9.refs_0_), channel_id=1, source_target_pairs={{0,1},{1,2},{2,3},{3,0},{4,5},{5,6},{6,7},{7,4},{8,9},{9,10},{10,1... | collective-permute-start | bytes 786440 | tf_op jit(solution)/shard_map/ppermute | solution.py:323
  89.5 42.6 %copy-start.31 = (bf16[32,4096]{1,0:T(8,128)(2,1)}, bf16[32,4096]{1,0:T(8,128)(2,1)S(1)}, u32[]{:S(2)}) copy-start(bf16[32,4096]{1,0:T(8,128)(2,1)S(1)} %collective-permute-done.12.refs_3_) | copy-start | bytes 786436
  89.5 23.8 %collective-permute-start.14 = (bf16[32,4096]{1,0:T(8,128)(2,1)S(1)}, bf16[32,4096]{1,0:T(8,128)(2,1)S(1)}, u32[]{:S(2)}, u32[]{:S(2)}) collective-permute-start(bf16[32,4096]{1,0:T(8,128)(2,1)S(1)} %collective-permute-done.12.refs_3_), channel_id=1, source_target_pairs={{0,3},{1,0},{2,1},{3,2},{4,7},{5,4},{6,5},{7,6},{8,11},{9,8},{10,9... | collective-permute-start | bytes 786440 | tf_op jit(solution)/shard_map/ppermute | solution.py:327
  108.9 38.7 %collective-permute-start.33 = (bf16[64,4096]{1,0:T(8,128)(2,1)}, bf16[64,4096]{1,0:T(8,128)(2,1)S(1)}, u32[]{:S(2)}, u32[]{:S(2)}) collective-permute-start(bf16[64,4096]{1,0:T(8,128)(2,1)} %get-tuple-element.60.refs_0_), channel_id=1, source_target_pairs={{0,1},{1,2},{2,3},{3,0},{4,5},{5,6},{6,7},{7,4},{8,9},{9,10},{10,1... | collective-permute-start | bytes 1572872 | tf_op jit(solution)/shard_map/ppermute | solution.py:323
  110.1 37.6 %collective-permute-start.36 = (bf16[64,4096]{1,0:T(8,128)(2,1)}, bf16[64,4096]{1,0:T(8,128)(2,1)S(1)}, u32[]{:S(2)}, u32[]{:S(2)}) collective-permute-start(bf16[64,4096]{1,0:T(8,128)(2,1)} %get-tuple-element.61.refs_1_), channel_id=1, source_target_pairs={{0,3},{1,0},{2,1},{3,2},{4,7},{5,4},{6,5},{7,6},{8,11},{9,8},{10,9... | collective-permute-start | bytes 1572872 | tf_op jit(solution)/shard_map/ppermute | solution.py:327
  110.9 19.8 %collective-permute-start.10 = (bf16[32,4096]{1,0:T(8,128)(2,1)}, bf16[32,4096]{1,0:T(8,128)(2,1)}, u32[]{:S(2)}, u32[]{:S(2)}) collective-permute-start(bf16[32,4096]{1,0:T(8,128)(2,1)} %get-tuple-element.39.refs_1_), channel_id=1, source_target_pairs={{0,1},{1,2},{2,3},{3,0},{4,5},{5,6},{6,7},{7,4},{8,9},{9,10},{10,1... | collective-permute-start | bytes 786440 | tf_op jit(solution)/shard_map/ppermute | solution.py:323
  113.3 18.8 %collective-permute-start.11 = (bf16[32,4096]{1,0:T(8,128)(2,1)}, bf16[32,4096]{1,0:T(8,128)(2,1)}, u32[]{:S(2)}, u32[]{:S(2)}) collective-permute-start(bf16[32,4096]{1,0:T(8,128)(2,1)} %get-tuple-element.38.refs_0_), channel_id=1, source_target_pairs={{0,3},{1,0},{2,1},{3,2},{4,7},{5,4},{6,5},{7,6},{8,11},{9,8},{10,9... | collective-permute-start | bytes 786440 | tf_op jit(solution)/shard_map/ppermute | solution.py:327
  122.5 22.0 %collective-permute-start.19 = (bf16[32,4096]{1,0:T(8,128)(2,1)}, bf16[32,4096]{1,0:T(8,128)(2,1)}, u32[]{:S(2)}, u32[]{:S(2)}) collective-permute-start(bf16[32,4096]{1,0:T(8,128)(2,1)} %get-tuple-element.47), channel_id=1, source_target_pairs={{0,3},{1,0},{2,1},{3,2},{4,7},{5,4},{6,5},{7,6},{8,11},{9,8},{10,9... | collective-permute-start | bytes 786440 | tf_op jit(solution)/shard_map/ppermute | solution.py:327
  125.1 65.4 %all-to-all-start.2 = ((bf16[64,8,1024]{2,1,0:T(8,128)(2,1)}), bf16[64,8,1024]{2,1,0:T(8,128)(2,1)S(1)}, u32[]{:S(2)}, u32[]{:S(2)}) async-start(bf16[64,8,1024]{2,1,0:T(8,128)(2,1)} %bitcast.11), calls=%async_computation.2 | async-start | bytes 2097152 | tf_op jit(solution)/shard_map/all_to_all | solution.py:332
  130.7 37.8 %copy-start.6 = (bf16[64,4096]{1,0:T(8,128)(2,1)S(1)}, bf16[64,4096]{1,0:T(8,128)(2,1)}, u32[]{:S(2)}) copy-start(bf16[64,4096]{1,0:T(8,128)(2,1)} %get-tuple-element.61.refs_1_) | copy-start | bytes 1572868
  141.1 38.3 %collective-permute-start.17 = (bf16[32,4096]{1,0:T(8,128)(2,1)}, bf16[32,4096]{1,0:T(8,128)(2,1)S(1)}, u32[]{:S(2)}, u32[]{:S(2)}) collective-permute-start(bf16[32,4096]{1,0:T(8,128)(2,1)} %get-tuple-element.43), channel_id=1, source_target_pairs={{0,3},{1,0},{2,1},{3,2},{4,7},{5,4},{6,5},{7,6},{8,11},{9,8},{10,9... | collective-permute-start | bytes 786440 | tf_op jit(solution)/shard_map/ppermute | solution.py:327
  143.0 38.2 %collective-permute-start.18 = (bf16[32,4096]{1,0:T(8,128)(2,1)}, bf16[32,4096]{1,0:T(8,128)(2,1)S(1)}, u32[]{:S(2)}, u32[]{:S(2)}) collective-permute-start(bf16[32,4096]{1,0:T(8,128)(2,1)} %get-tuple-element.45), channel_id=1, source_target_pairs={{0,1},{1,2},{2,3},{3,0},{4,5},{5,6},{6,7},{7,4},{8,9},{9,10},{10,1... | collective-permute-start | bytes 786440 | tf_op jit(solution)/shard_map/ppermute | solution.py:323
  144.4 35.4 %collective-permute-start.15 = (bf16[32,4096]{1,0:T(8,128)(2,1)S(1)}, bf16[32,4096]{1,0:T(8,128)(2,1)S(1)}, u32[]{:S(2)}, u32[]{:S(2)}) collective-permute-start(bf16[32,4096]{1,0:T(8,128)(2,1)S(1)} %copy-done.45), channel_id=1, source_target_pairs={{0,1},{1,2},{2,3},{3,0},{4,5},{5,6},{6,7},{7,4},{8,9},{9,10},{10,1... | collective-permute-start | bytes 786440 | tf_op jit(solution)/shard_map/ppermute | solution.py:323
  147.6 31.8 %copy-start.8 = (bf16[64,4096]{1,0:T(8,128)(2,1)}, bf16[64,4096]{1,0:T(8,128)(2,1)S(1)}, u32[]{:S(2)}) copy-start(bf16[64,4096]{1,0:T(8,128)(2,1)S(1)} %collective-permute-done.33.refs_0_) | copy-start | bytes 1572868
  147.6 20.5 %collective-permute-start.37 = (bf16[64,4096]{1,0:T(8,128)(2,1)S(1)}, bf16[64,4096]{1,0:T(8,128)(2,1)S(1)}, u32[]{:S(2)}, u32[]{:S(2)}) collective-permute-start(bf16[64,4096]{1,0:T(8,128)(2,1)S(1)} %collective-permute-done.33.refs_0_), channel_id=1, source_target_pairs={{0,1},{1,2},{2,3},{3,0},{4,5},{5,6},{6,7},{7,4},{8,9},{9,10},{10,1... | collective-permute-start | bytes 1572872 | tf_op jit(solution)/shard_map/ppermute | solution.py:323
  147.7 31.7 %copy-start.9 = (bf16[64,4096]{1,0:T(8,128)(2,1)}, bf16[64,4096]{1,0:T(8,128)(2,1)S(1)}, u32[]{:S(2)}) copy-start(bf16[64,4096]{1,0:T(8,128)(2,1)S(1)} %collective-permute-done.36.refs_3_) | copy-start | bytes 1572868
  147.7 20.7 %collective-permute-start.38 = (bf16[64,4096]{1,0:T(8,128)(2,1)S(1)}, bf16[64,4096]{1,0:T(8,128)(2,1)S(1)}, u32[]{:S(2)}, u32[]{:S(2)}) collective-permute-start(bf16[64,4096]{1,0:T(8,128)(2,1)S(1)} %collective-permute-done.36.refs_3_), channel_id=1, source_target_pairs={{0,3},{1,0},{2,1},{3,2},{4,7},{5,4},{6,5},{7,6},{8,11},{9,8},{10,9... | collective-permute-start | bytes 1572872 | tf_op jit(solution)/shard_map/ppermute | solution.py:327
  151.4 27.9 %copy-start.5 = (bf16[64,4096]{1,0:T(8,128)(2,1)S(1)}, bf16[64,4096]{1,0:T(8,128)(2,1)}, u32[]{:S(2)}) copy-start(bf16[64,4096]{1,0:T(8,128)(2,1)} %get-tuple-element.60.refs_0_) | copy-start | bytes 1572868
  151.4 29.7 %copy-start.30 = (bf16[32,4096]{1,0:T(8,128)(2,1)S(1)}, bf16[32,4096]{1,0:T(8,128)(2,1)}, u32[]{:S(2)}) copy-start(bf16[32,4096]{1,0:T(8,128)(2,1)} %get-tuple-element.41) | copy-start | bytes 786436
  168.1 26.1 %collective-permute-start.20 = (bf16[32,4096]{1,0:T(8,128)(2,1)}, bf16[32,4096]{1,0:T(8,128)(2,1)}, u32[]{:S(2)}, u32[]{:S(2)}) collective-permute-start(bf16[32,4096]{1,0:T(8,128)(2,1)} %add_convert_fusion.4), channel_id=1, source_target_pairs={{0,3},{1,0},{2,1},{3,2},{4,7},{5,4},{6,5},{7,6},{8,11},{9,8},{10,9... | collective-permute-start | bytes 786440 | tf_op jit(solution)/shard_map/ppermute | solution.py:327
  168.4 41.8 %collective-permute-start.34 = (bf16[64,4096]{1,0:T(8,128)(2,1)S(1)}, bf16[64,4096]{1,0:T(8,128)(2,1)}, u32[]{:S(2)}, u32[]{:S(2)}) collective-permute-start(bf16[64,4096]{1,0:T(8,128)(2,1)S(1)} %copy-done.6), channel_id=1, source_target_pairs={{0,1},{1,2},{2,3},{3,0},{4,5},{5,6},{6,7},{7,4},{8,9},{9,10},{10,1... | collective-permute-start | bytes 1572872 | tf_op jit(solution)/shard_map/ppermute | solution.py:323
  179.4 34.1 %collective-permute-start.35 = (bf16[64,4096]{1,0:T(8,128)(2,1)S(1)}, bf16[64,4096]{1,0:T(8,128)(2,1)}, u32[]{:S(2)}, u32[]{:S(2)}) collective-permute-start(bf16[64,4096]{1,0:T(8,128)(2,1)S(1)} %copy-done.5), channel_id=1, source_target_pairs={{0,3},{1,0},{2,1},{3,2},{4,7},{5,4},{6,5},{7,6},{8,11},{9,8},{10,9... | collective-permute-start | bytes 1572872 | tf_op jit(solution)/shard_map/ppermute | solution.py:327
  179.8 44.4 %collective-permute-start.43 = (bf16[64,4096]{1,0:T(8,128)(2,1)}, bf16[64,4096]{1,0:T(8,128)(2,1)}, u32[]{:S(2)}, u32[]{:S(2)}) collective-permute-start(bf16[64,4096]{1,0:T(8,128)(2,1)} %get-tuple-element.69), channel_id=1, source_target_pairs={{0,3},{1,0},{2,1},{3,2},{4,7},{5,4},{6,5},{7,6},{8,11},{9,8},{10,9... | collective-permute-start | bytes 1572872 | tf_op jit(solution)/shard_map/ppermute | solution.py:327
  181.2 15.3 %collective-permute-start.16 = (bf16[32,4096]{1,0:T(8,128)(2,1)S(1)}, bf16[32,4096]{1,0:T(8,128)(2,1)}, u32[]{:S(2)}, u32[]{:S(2)}) collective-permute-start(bf16[32,4096]{1,0:T(8,128)(2,1)S(1)} %add_convert_fusion.5), channel_id=1, source_target_pairs={{0,1},{1,2},{2,3},{3,0},{4,5},{5,6},{6,7},{7,4},{8,9},{9,10},{10,1... | collective-permute-start | bytes 786440 | tf_op jit(solution)/shard_map/ppermute | solution.py:323
  194.2 33.6 %collective-permute-start.24 = (bf16[64,4096]{1,0:T(8,128)(2,1)}, bf16[64,4096]{1,0:T(8,128)(2,1)S(1)}, u32[]{:S(2)}, u32[]{:S(2)}) collective-permute-start(bf16[64,4096]{1,0:T(8,128)(2,1)} %get-tuple-element.50.refs_1_), channel_id=1, source_target_pairs={{0,3},{1,0},{2,1},{3,2},{4,7},{5,4},{6,5},{7,6},{8,11},{9,8},{10,9... | collective-permute-start | bytes 1572872 | tf_op jit(solution)/shard_map/ppermute | solution.py:327
  196.5 44.7 %collective-permute-start.22 = (bf16[64,4096]{1,0:T(8,128)(2,1)}, bf16[64,4096]{1,0:T(8,128)(2,1)S(1)}, u32[]{:S(2)}, u32[]{:S(2)}) collective-permute-start(bf16[64,4096]{1,0:T(8,128)(2,1)} %get-tuple-element.50.refs_1_), channel_id=1, source_target_pairs={{0,1},{1,2},{2,3},{3,0},{4,5},{5,6},{6,7},{7,4},{8,9},{9,10},{10,1... | collective-permute-start | bytes 1572872 | tf_op jit(solution)/shard_map/ppermute | solution.py:323
  199.8 95.7 %all-to-all-start.1 = ((bf16[64,8,512]{2,1,0:T(8,128)(2,1)}), bf16[64,8,512]{2,1,0:T(8,128)(2,1)S(1)}, u32[]{:S(2)}, u32[]{:S(2)}) async-start(bf16[64,8,512]{2,1,0:T(8,128)(2,1)} %bitcast.56), calls=%async_computation.1 | async-start | bytes 1048576 | tf_op jit(solution)/shard_map/all_to_all | solution.py:332
  210.2 17.4 %collective-permute-start.21 = (bf16[64,4096]{1,0:T(8,128)(2,1)S(1)}, bf16[64,4096]{1,0:T(8,128)(2,1)S(1)}, u32[]{:S(2)}, u32[]{:S(2)}) collective-permute-start(bf16[64,4096]{1,0:T(8,128)(2,1)S(1)} %copy-done.7), channel_id=1, source_target_pairs={{0,1},{1,2},{2,3},{3,0},{4,5},{5,6},{6,7},{7,4},{8,9},{9,10},{10,1... | collective-permute-start | bytes 1572872 | tf_op jit(solution)/shard_map/ppermute | solution.py:323
  213.5 52.3 %collective-permute-start.23 = (bf16[64,4096]{1,0:T(8,128)(2,1)S(1)}, bf16[64,4096]{1,0:T(8,128)(2,1)S(1)}, u32[]{:S(2)}, u32[]{:S(2)}) collective-permute-start(bf16[64,4096]{1,0:T(8,128)(2,1)S(1)} %copy-done.7), channel_id=1, source_target_pairs={{0,3},{1,0},{2,1},{3,2},{4,7},{5,4},{6,5},{7,6},{8,11},{9,8},{10,9... | collective-permute-start | bytes 1572872 | tf_op jit(solution)/shard_map/ppermute | solution.py:327
  224.2 17.0 %copy-start.44 = (bf16[64,4096]{1,0:T(8,128)(2,1)S(1)}, bf16[64,4096]{1,0:T(8,128)(2,1)}, u32[]{:S(2)}) copy-start(bf16[64,4096]{1,0:T(8,128)(2,1)} %get-tuple-element.67) | copy-start | bytes 1572868
  224.3 14.9 %collective-permute-start.39 = (bf16[64,4096]{1,0:T(8,128)(2,1)S(1)}, bf16[64,4096]{1,0:T(8,128)(2,1)S(1)}, u32[]{:S(2)}, u32[]{:S(2)}) collective-permute-start(bf16[64,4096]{1,0:T(8,128)(2,1)S(1)} %copy-done.43), channel_id=1, source_target_pairs={{0,1},{1,2},{2,3},{3,0},{4,5},{5,6},{6,7},{7,4},{8,9},{9,10},{10,1... | collective-permute-start | bytes 1572872 | tf_op jit(solution)/shard_map/ppermute | solution.py:323
  227.7 38.0 %copy-start.12 = (bf16[64,4096]{1,0:T(8,128)(2,1)}, bf16[64,4096]{1,0:T(8,128)(2,1)S(1)}, u32[]{:S(2)}) copy-start(bf16[64,4096]{1,0:T(8,128)(2,1)S(1)} %collective-permute-done.21.refs_0_) | copy-start | bytes 1572868
  227.7 58.0 %collective-permute-start.41 = (bf16[64,4096]{1,0:T(8,128)(2,1)}, bf16[64,4096]{1,0:T(8,128)(2,1)S(1)}, u32[]{:S(2)}, u32[]{:S(2)}) collective-permute-start(bf16[64,4096]{1,0:T(8,128)(2,1)} %get-tuple-element.65), channel_id=1, source_target_pairs={{0,3},{1,0},{2,1},{3,2},{4,7},{5,4},{6,5},{7,6},{8,11},{9,8},{10,9... | collective-permute-start | bytes 1572872 | tf_op jit(solution)/shard_map/ppermute | solution.py:327
  227.8 37.9 %copy-start.10 = (bf16[64,4096]{1,0:T(8,128)(2,1)}, bf16[64,4096]{1,0:T(8,128)(2,1)S(1)}, u32[]{:S(2)}) copy-start(bf16[64,4096]{1,0:T(8,128)(2,1)S(1)} %collective-permute-done.24.refs_3_) | copy-start | bytes 1572868
  227.8 22.6 %collective-permute-start.25 = (bf16[64,4096]{1,0:T(8,128)(2,1)S(1)}, bf16[64,4096]{1,0:T(8,128)(2,1)S(1)}, u32[]{:S(2)}, u32[]{:S(2)}) collective-permute-start(bf16[64,4096]{1,0:T(8,128)(2,1)S(1)} %collective-permute-done.21.refs_0_), channel_id=1, source_target_pairs={{0,1},{1,2},{2,3},{3,0},{4,5},{5,6},{6,7},{7,4},{8,9},{9,10},{10,1... | collective-permute-start | bytes 1572872 | tf_op jit(solution)/shard_map/ppermute | solution.py:323
  239.2 14.6 %collective-permute-start.26 = (bf16[64,4096]{1,0:T(8,128)(2,1)S(1)}, bf16[64,4096]{1,0:T(8,128)(2,1)S(1)}, u32[]{:S(2)}, u32[]{:S(2)}) collective-permute-start(bf16[64,4096]{1,0:T(8,128)(2,1)S(1)} %collective-permute-done.24.refs_3_), channel_id=1, source_target_pairs={{0,3},{1,0},{2,1},{3,2},{4,7},{5,4},{6,5},{7,6},{8,11},{9,8},{10,9... | collective-permute-start | bytes 1572872 | tf_op jit(solution)/shard_map/ppermute | solution.py:327
  241.2 24.5 %copy-start.11 = (bf16[64,4096]{1,0:T(8,128)(2,1)}, bf16[64,4096]{1,0:T(8,128)(2,1)S(1)}, u32[]{:S(2)}) copy-start(bf16[64,4096]{1,0:T(8,128)(2,1)S(1)} %collective-permute-done.22.refs_1_) | copy-start | bytes 1572868
  241.2 44.6 %collective-permute-start.42 = (bf16[64,4096]{1,0:T(8,128)(2,1)S(1)}, bf16[64,4096]{1,0:T(8,128)(2,1)S(1)}, u32[]{:S(2)}, u32[]{:S(2)}) collective-permute-start(bf16[64,4096]{1,0:T(8,128)(2,1)S(1)} %copy-done.44), channel_id=1, source_target_pairs={{0,1},{1,2},{2,3},{3,0},{4,5},{5,6},{6,7},{7,4},{8,9},{9,10},{10,1... | collective-permute-start | bytes 1572872 | tf_op jit(solution)/shard_map/ppermute | solution.py:323
  250.4 37.4 %collective-permute-start.44 = (bf16[64,4096]{1,0:T(8,128)(2,1)S(1)}, bf16[64,4096]{1,0:T(8,128)(2,1)S(1)}, u32[]{:S(2)}, u32[]{:S(2)}) collective-permute-start(bf16[64,4096]{1,0:T(8,128)(2,1)S(1)} %add_convert_fusion), channel_id=1, source_target_pairs={{0,3},{1,0},{2,1},{3,2},{4,7},{5,4},{6,5},{7,6},{8,11},{9,8},{10,9... | collective-permute-start | bytes 1572872 | tf_op jit(solution)/shard_map/ppermute | solution.py:327
  253.8 37.2 %collective-permute-start.40 = (bf16[64,4096]{1,0:T(8,128)(2,1)S(1)}, bf16[64,4096]{1,0:T(8,128)(2,1)S(1)}, u32[]{:S(2)}, u32[]{:S(2)}) collective-permute-start(bf16[64,4096]{1,0:T(8,128)(2,1)S(1)} %add_convert_fusion.1), channel_id=1, source_target_pairs={{0,1},{1,2},{2,3},{3,0},{4,5},{5,6},{6,7},{7,4},{8,9},{9,10},{10,1... | collective-permute-start | bytes 1572872 | tf_op jit(solution)/shard_map/ppermute | solution.py:323
  265.8 40.1 %collective-permute-start.31 = (bf16[64,4096]{1,0:T(8,128)(2,1)}, bf16[64,4096]{1,0:T(8,128)(2,1)S(1)}, u32[]{:S(2)}, u32[]{:S(2)}) collective-permute-start(bf16[64,4096]{1,0:T(8,128)(2,1)} %get-tuple-element.58), channel_id=1, source_target_pairs={{0,3},{1,0},{2,1},{3,2},{4,7},{5,4},{6,5},{7,6},{8,11},{9,8},{10,9... | collective-permute-start | bytes 1572872 | tf_op jit(solution)/shard_map/ppermute | solution.py:327
  285.7 34.0 %collective-permute-start.29 = (bf16[64,4096]{1,0:T(8,128)(2,1)}, bf16[64,4096]{1,0:T(8,128)(2,1)}, u32[]{:S(2)}, u32[]{:S(2)}) collective-permute-start(bf16[64,4096]{1,0:T(8,128)(2,1)} %get-tuple-element.54), channel_id=1, source_target_pairs={{0,3},{1,0},{2,1},{3,2},{4,7},{5,4},{6,5},{7,6},{8,11},{9,8},{10,9... | collective-permute-start | bytes 1572872 | tf_op jit(solution)/shard_map/ppermute | solution.py:327
  285.8 33.9 %collective-permute-start.30 = (bf16[64,4096]{1,0:T(8,128)(2,1)}, bf16[64,4096]{1,0:T(8,128)(2,1)}, u32[]{:S(2)}, u32[]{:S(2)}) collective-permute-start(bf16[64,4096]{1,0:T(8,128)(2,1)} %get-tuple-element.56), channel_id=1, source_target_pairs={{0,1},{1,2},{2,3},{3,0},{4,5},{5,6},{6,7},{7,4},{8,9},{9,10},{10,1... | collective-permute-start | bytes 1572872 | tf_op jit(solution)/shard_map/ppermute | solution.py:323
  287.8 20.6 %collective-permute-start.27 = (bf16[64,4096]{1,0:T(8,128)(2,1)}, bf16[64,4096]{1,0:T(8,128)(2,1)}, u32[]{:S(2)}, u32[]{:S(2)}) collective-permute-start(bf16[64,4096]{1,0:T(8,128)(2,1)} %get-tuple-element.53), channel_id=1, source_target_pairs={{0,1},{1,2},{2,3},{3,0},{4,5},{5,6},{6,7},{7,4},{8,9},{9,10},{10,1... | collective-permute-start | bytes 1572872 | tf_op jit(solution)/shard_map/ppermute | solution.py:323
  291.8 16.6 %copy-start.14 = (bf16[64,4096]{1,0:T(8,128)(2,1)S(1)}, bf16[64,4096]{1,0:T(8,128)(2,1)}, u32[]{:S(2)}) copy-start(bf16[64,4096]{1,0:T(8,128)(2,1)} %get-tuple-element.52) | copy-start | bytes 1572868
  295.5 24.2 %copy-start.4 = (bf16[64,8,512]{2,1,0:T(8,128)(2,1)}, bf16[64,8,512]{2,1,0:T(8,128)(2,1)S(1)}, u32[]{:S(2)}) copy-start(bf16[64,8,512]{2,1,0:T(8,128)(2,1)S(1)} %all-to-all-done.1) | copy-start | bytes 1572868
  295.5 39.3 %all-to-all-start.5 = ((bf16[64,8,1024]{2,1,0:T(8,128)(2,1)}), bf16[64,8,1024]{2,1,0:T(8,128)(2,1)S(1)}, u32[]{:S(2)}, u32[]{:S(2)}) async-start(bf16[64,8,1024]{2,1,0:T(8,128)(2,1)} %bitcast.52), calls=%async_computation.5 | async-start | bytes 2097152 | tf_op jit(solution)/shard_map/all_to_all | solution.py:332
  306.1 14.0 %collective-permute-start.32 = (bf16[64,4096]{1,0:T(8,128)(2,1)S(1)}, bf16[64,4096]{1,0:T(8,128)(2,1)S(1)}, u32[]{:S(2)}, u32[]{:S(2)}) collective-permute-start(bf16[64,4096]{1,0:T(8,128)(2,1)S(1)} %add_convert_fusion.2), channel_id=1, source_target_pairs={{0,3},{1,0},{2,1},{3,2},{4,7},{5,4},{6,5},{7,6},{8,11},{9,8},{10,9... | collective-permute-start | bytes 1572872 | tf_op jit(solution)/shard_map/ppermute | solution.py:327
  309.5 12.0 %collective-permute-start.28 = (bf16[64,4096]{1,0:T(8,128)(2,1)S(1)}, bf16[64,4096]{1,0:T(8,128)(2,1)S(1)}, u32[]{:S(2)}, u32[]{:S(2)}) collective-permute-start(bf16[64,4096]{1,0:T(8,128)(2,1)S(1)} %add_convert_fusion.3), channel_id=1, source_target_pairs={{0,1},{1,2},{2,3},{3,0},{4,5},{5,6},{6,7},{7,4},{8,9},{9,10},{10,1... | collective-permute-start | bytes 1572872 | tf_op jit(solution)/shard_map/ppermute | solution.py:323
  334.8 34.6 %copy-start.1 = (bf16[64,8,1024]{2,1,0:T(8,128)(2,1)}, bf16[64,8,1024]{2,1,0:T(8,128)(2,1)S(1)}, u32[]{:S(2)}) copy-start(bf16[64,8,1024]{2,1,0:T(8,128)(2,1)S(1)} %all-to-all-done.5) | copy-start | bytes 3145732
  (31 other events, 165.7 us)

commit v2 on v1

--- a/solution.py
+++ b/solution.py
@@ -158,60 +158,46 @@
     )(user, sp, stream, base, *keys, *values, *adapters, gain_a, gain_e, routes)
 
 
-def blocks_of(n):
-    half = n * EXPERTS // 2
+def arrive_kernel(n, received, out):
+    rows = one_hot_dot(from_segments(), received[...])
     for c in range(n):
-        lo, hi = c * EXPERTS, (c + 1) * EXPERTS
-        for which, (a, b) in enumerate(((0, half), (half, 2 * half))):
-            x, y = max(lo, a), min(hi, b)
-            if x < y:
-                yield c, which, x - a, x - lo, y - x
-
-
-def arrive_kernel(n, received, *halves):
-    rows = one_hot_dot(from_segments(), received[...])
-    for c, which, to, at, size in blocks_of(n):
         for s in range(SEG):
-            halves[which][to : to + size, s * WIDE : (s + 1) * WIDE] = rows[
-                s * EXPERTS + at : s * EXPERTS + at + size, c * WIDE : (c + 1) * WIDE
+            out[c * EXPERTS : (c + 1) * EXPERTS, s * WIDE : (s + 1) * WIDE] = rows[
+                s * EXPERTS : (s + 1) * EXPERTS, c * WIDE : (c + 1) * WIDE
             ]
 
 
 def arrive(n, received):
-    half = jax.ShapeDtypeStruct((n * EXPERTS // 2, D), bf16)
     return pl.pallas_call(
         functools.partial(arrive_kernel, n),
-        out_shape=[half, half],
+        out_shape=jax.ShapeDtypeStruct((n * EXPERTS, D), bf16),
         in_specs=[VMEM_SPEC],
-        out_specs=[VMEM_SPEC] * 2,
+        out_specs=VMEM_SPEC,
         compiler_params=PARAMS,
         name="arrive",
     )(received)
 
 
-def leave_kernel(n, *refs):
-    terms, out, stack = (refs[0:3], refs[3:6]), refs[6], refs[7]
-    for c, which, at, to, size in blocks_of(n):
+def leave_kernel(n, own, other, last, out, stack):
+    for c in range(n):
         for s in range(SEG):
-            cols = slice(s * WIDE, (s + 1) * WIDE)
-            total = sum(t[at : at + size, cols].astype(f32) for t in terms[which])
-            stack[
-                s * EXPERTS + to : s * EXPERTS + to + size, c * WIDE : (c + 1) * WIDE
-            ] = total.astype(bf16)
+            at = slice(c * EXPERTS, (c + 1) * EXPERTS), slice(s * WIDE, (s + 1) * WIDE)
+            total = own[at].astype(f32) + other[at].astype(f32) + last[at].astype(f32)
+            stack[s * EXPERTS : (s + 1) * EXPERTS, c * WIDE : (c + 1) * WIDE] = total.astype(bf16)
     out[...] = one_hot_dot(to_segments(), stack[...])
 
 
-def leave(n, terms_a, terms_b):
+def leave(n, *terms):
     shape = (EXPERTS * SEG, n * WIDE)
     return pl.pallas_call(
         functools.partial(leave_kernel, n),
         out_shape=jax.ShapeDtypeStruct(shape, bf16),
-        in_specs=[VMEM_SPEC] * 6,
+        in_specs=[VMEM_SPEC] * 3,
         out_specs=VMEM_SPEC,
         scratch_shapes=[pltpu.VMEM(shape, bf16)],
         compiler_params=PARAMS,
         name="leave",
-    )(*terms_a, *terms_b)
+    )(*terms)
 
 
 STEPS = 4
@@ -222,7 +208,6 @@
     outs = refs[n + 3 : 2 * n + 3]
     gate_sum, up_sum, act = refs[2 * n + 3 :]
     i = pl.program_id(0)
-    depth = D // STEPS
 
     @pl.when(i == 0)
     def _():
@@ -231,8 +216,7 @@
 
     @pl.when(i < STEPS)
     def _():
-        cols = pl.ds(pl.multiple_of(i * depth, depth), depth)
-        x = jnp.concatenate([r[:, cols] for r in rows], axis=0)
+        x = jnp.concatenate([r[...] for r in rows], axis=0)
         gate_sum[...] += dot(x, gate[...])
         up_sum[...] += dot(x, up[...])
 
@@ -259,7 +243,7 @@
         functools.partial(expert_kernel, n),
         out_shape=[jax.ShapeDtypeStruct((size, D), bf16)] * n,
         grid=(2 * STEPS,),
-        in_specs=[pl.BlockSpec((size, D), lambda i: (0, 0))] * n
+        in_specs=[pl.BlockSpec((size, depth), lambda i: (0, jnp.minimum(i, STEPS - 1)))] * n
         + [pl.BlockSpec((depth, hidden), first)] * 2
         + [pl.BlockSpec((hidden, depth), last)],
         out_specs=[pl.BlockSpec((size, depth), last)] * n,
@@ -327,28 +311,57 @@
     return lax.ppermute(x, "sp", [(i, (i + 3) % 4) for i in range(4)])
 
 
+def across(x):
+    return lax.ppermute(x, "sp", [(i, (i + 2) % 4) for i in range(4)])
+
+
 def exchange(x, n):
     cut = x.reshape(EXPERTS, SEG, n * WIDE)
     moved = lax.all_to_all(cut, "ep", split_axis=0, concat_axis=0, tiled=True)
     return moved.reshape(EXPERTS * SEG, n * WIDE)
 
 
-def feed_forward(n, sent, gate, up, down):
-    a, b = arrive(n, exchange(sent, n))
-    a_left, a_right = right(a), left(a)
-    b_left, b_right = right(b), left(b)
-    a_far, b_far = right(a_left), left(b_right)
-    pa_far, pb_far = expert([a_far, b_far], gate, up, down)
-    a_in, b_in = right(pa_far), left(pb_far)
-    pa_left, pb_left, pa_right, pb_right = expert(
-        [a_left, b_left, a_right, b_right], gate, up, down
-    )
-    pa, pb = expert([a, b], gate, up, down)
-    add = lambda x, y: (x.astype(f32) + y.astype(f32)).astype(bf16)
-    a_from_left, b_from_left = right(add(pa_right, a_in)), right(pb_right)
-    a_from_right, b_from_right = left(pa_left), left(add(pb_left, b_in))
-    out = leave(n, (pa, a_from_left, a_from_right), (pb, b_from_left, b_from_right))
-    return exchange(out, n)
+def after(x, *others):
+    return lax.optimization_barrier((x, *others))[0]
+
+
+def feed_forward(sends, gate, up, down):
+    count = len(CHUNKS)
+    first = exchange(sends[0], CHUNKS[0])
+    second = exchange(after(sends[1], first), CHUNKS[1])
+    arrived = [first, second]
+    ways = [(right, left) if c % 2 == 0 else (left, right) for c in range(count)]
+    pieces, parts = [], []
+    for c, n in enumerate(CHUNKS):
+        ahead, back = ways[c]
+        x = arrived[c]
+        if c == 0:
+            own = arrive(n, x)
+            behind, front, far = ahead(own), back(own), across(own)
+        else:
+            _, _, front_before, far_before = pieces[-1]
+            own = arrive(n, x if c == 1 else after(x, parts[-1][0]))
+            behind = ahead(own if c == 1 else after(own, front_before))
+            front = back(own if c == 1 else after(own, far_before))
+            parts.append(expert(pieces[-1], gate, up, down))
+            far = ahead(after(behind, parts[-1][0]) if c == 1 else behind)
+        pieces.append((own, behind, front, far))
+        if c + 2 < count:
+            ready = after(sends[c + 2], arrived[c + 1], behind, front, far)
+            arrived.append(exchange(ready, CHUNKS[c + 2]))
+    parts.append(expert(pieces[-1], gate, up, down))
+    returned, done = [], None
+    for c, n in enumerate(CHUNKS):
+        ahead, back = ways[c]
+        p_own, p_behind, p_front, p_far = parts[c]
+        if c + 1 < count:
+            p_far = after(p_far, pieces[c + 1][1])
+        passed = back(p_far)
+        whole = (p_behind.astype(f32) + passed.astype(f32)).astype(bf16)
+        out = leave(n, p_own, ahead(p_front), back(whole))
+        done = exchange(out if done is None else after(out, done), n)
+        returned.append(done)
+    return returned
 
 
 def on_device(
@@ -397,7 +410,7 @@
         routes_t,
     )
     gate, up, down = gate_weight[0], up_weight[0], down_weight[0]
-    received = [feed_forward(n, x, gate, up, down) for n, x in zip(CHUNKS, sends)]
+    received = feed_forward(sends, gate, up, down)
     moe_out = combine(sp, routes_t, weights_t, received, stream.shape[0])
     return (hidden, moe_out)
 

time: 382 us -> 358 us (0.937)
  the two profiles are of different devices: /device:TPU:4 before, /device:TPU:6 now
where the time goes in v2:
time: 358 us; the launch traced here: 351 us
  waiting for transfers between devices  122 us (34%)
  starting transfers between devices  73.8 us (21%)
  Pallas kernels  72.3 us (20%)
  blocking collectives  70.1 us (20%)
  local copies, waits for them, and re-layouts  8.18 us (2%)
    all_to_all x2, blocking collectives, exchange(): moved = lax.all_to_all(cut, 'ep', split_axis=0, concat_axis=0, tiled=True)  70.1 us
    ppermute x13, waiting for transfers between devices, left(): return lax.ppermute(x, 'sp', [(i, (i + 3) % 4) for i in range(4)])  63.8 us
    ppermute x13, waiting for transfers between devices, right(): return lax.ppermute(x, 'sp', [(i, (i + 1) % 4) for i in range(4)])  46.1 us
    all_to_all x4, starting transfers between devices, exchange(): moved = lax.all_to_all(cut, 'ep', split_axis=0, concat_axis=0, tiled=True)  37.2 us
    pallas_call x3, Pallas kernels, expert(): pl.pallas_call(functools.partial(expert_kernel, n), out_shape=[jax.ShapeD...  36.6 us
    ppermute x13, starting transfers between devices, right(): return lax.ppermute(x, 'sp', [(i, (i + 1) % 4) for i in range(4)])  28.2 us
    pallas_call x1, Pallas kernels, attention(): pl.pallas_call(attention_kernel, out_shape=outs, in_specs=[SMEM_SPEC] * 2...  12 us
    ppermute x1, waiting for transfers between devices, across(): return lax.ppermute(x, 'sp', [(i, (i + 2) % 4) for i in range(4)])  11.7 us
  transfers between devices with their start and end apart: 31, of which 12 were waited for; matrix products, arithmetic and copies ran while one was open for 2% of the time, Pallas kernels for 16%

profile of v2, /device:TPU:6, one launch (start us, length us, event | category | flops | bytes accessed | tf_op | source)
XLA Modules:
  0.0 351.2 jit_solution(2611772435106159487)
XLA Ops:
  0.6 2.3 collective-permute-start
  3.6 0.2 convolution_convert_fusion.1
  3.8 1.2 convolution_convert_fusion
  5.1 0.7 collective-permute-start.7
  5.8 2.7 collective-permute-start.6
  8.5 7.6 %collective-permute-done.7.refs_10_ = bf16[64,1024]{1,0:T(8,128)(2,1)S(1)} collective-permute-done((bf16[64,1024]{1,0:T(8,128)(2,1)S(1)}, bf16[64,1024]{1,0:T(8,128)(2,1)S(1)}, u32[]{:S(2)}, u32[]{:S(2)}) %collective-permute-start.7) | collective-permute-done | bytes 131104 | tf_op jit(solution)/shard_map/ppermute | solution.py:311
  16.1 0.3 collective-permute-start.2
  16.4 1.8 collective-permute-start.5
  18.2 1.6 collective-permute-start.8
  19.8 1.3 reshape.56.refs_12_
  21.2 1.3 reshape.57.refs_13_
  22.5 5.3 %collective-permute-done.8.refs_11_ = bf16[64,1024]{1,0:T(8,128)(2,1)S(1)} collective-permute-done((bf16[64,1024]{1,0:T(8,128)(2,1)S(1)}, bf16[64,1024]{1,0:T(8,128)(2,1)S(1)}, u32[]{:S(2)}, u32[]{:S(2)}) %collective-permute-start.8) | collective-permute-done | bytes 131104 | tf_op jit(solution)/shard_map/ppermute | solution.py:307
  27.9 0.5 copy-done.26
  28.5 0.1 copy-done.20
  28.6 0.1 copy-done.22
  28.7 0.1 copy-done.23
  28.8 12.0 %attention.1 = (bf16[128,4096]{1,0:T(8,128)(2,1)}, bf16[512,512]{1,0:T(8,128)(2,1)}, bf16[512,1024]{1,0:T(8,128)(2,1)}, bf16[512,1024]{1,0:T(8,128)(2,1)}) custom-call(s32[1]{0:T(128)S(6)} %copy.16.user_ref, s32[1]{0:T(128)} %bitcast.sp_ref, bf16[128,4096]{1,0:T(8,128)(2,1)} %stream.1, bf16[128,4096]{1,0:T(8,128)(2,1)} %base.1, bf16[128,1024]{1,0:T(8,128)(2,1)} %refs_0_.1, ...), custom_call_target="tpu_custom_call" | custom-call | tf_op jit(solution)/shard_map/attention/pallas_call | solution.py:146
  40.8 30.8 %all_to_all.30 = bf16[64,8,512]{2,1,0:T(8,128)(2,1)} all-to-all(bf16[64,8,512]{2,1,0:T(8,128)(2,1)} %bitcast.40), channel_id=1, replica_groups=mesh['ep'=64,'sp'=4] {'ep'}, dimensions={0} | all-to-all | bytes 1048576 | tf_op jit(solution)/shard_map/all_to_all | solution.py:320
  71.6 5.8 %all-to-all-start.1 = ((bf16[64,8,1024]{2,1,0:T(8,128)(2,1)}), bf16[64,8,1024]{2,1,0:T(8,128)(2,1)S(1)}, u32[]{:S(2)}, u32[]{:S(2)}) async-start(bf16[64,8,1024]{2,1,0:T(8,128)(2,1)} %bitcast.39), calls=%async_computation.1 | async-start | bytes 2097152 | tf_op jit(solution)/shard_map/all_to_all | solution.py:320
  77.4 2.3 arrive.3.refs_0_
  79.7 1.2 collective-permute-start.11
  80.9 1.2 collective-permute-start.10
  82.0 2.4 collective-permute-start.9
  84.5 11.7 %collective-permute-done.11.refs_3_ = bf16[64,4096]{1,0:T(8,128)(2,1)S(1)} collective-permute-done((bf16[64,4096]{1,0:T(8,128)(2,1)}, bf16[64,4096]{1,0:T(8,128)(2,1)S(1)}, u32[]{:S(2)}, u32[]{:S(2)}) %collective-permute-start.11) | collective-permute-done | bytes 524320 | tf_op jit(solution)/shard_map/ppermute | solution.py:315
  96.2 10.3 %collective-permute-done.10.refs_2_ = bf16[64,4096]{1,0:T(8,128)(2,1)S(1)} collective-permute-done((bf16[64,4096]{1,0:T(8,128)(2,1)}, bf16[64,4096]{1,0:T(8,128)(2,1)S(1)}, u32[]{:S(2)}, u32[]{:S(2)}) %collective-permute-start.10) | collective-permute-done | bytes 524320 | tf_op jit(solution)/shard_map/ppermute | solution.py:311
  106.5 0.8 copy-done.14
  107.4 10.4 %all-to-all-start.3 = ((bf16[64,8,1024]{2,1,0:T(8,128)(2,1)}), bf16[64,8,1024]{2,1,0:T(8,128)(2,1)S(1)}, u32[]{:S(2)}, u32[]{:S(2)}) async-start(bf16[64,8,1024]{2,1,0:T(8,128)(2,1)} %bitcast.13), calls=%async_computation.3 | async-start | bytes 2097152 | tf_op jit(solution)/shard_map/all_to_all | solution.py:320
  117.8 2.9 arrive.4.refs_0_
  120.7 0.3 collective-permute-start.13
  121.0 2.9 collective-permute-start.16
  123.9 10.2 %expert.3 = (bf16[64,4096]{1,0:T(8,128)(2,1)}, bf16[64,4096]{1,0:T(8,128)(2,1)}, bf16[64,4096]{1,0:T(8,128)(2,1)}, bf16[64,4096]{1,0:T(8,128)(2,1)}) custom-call(bf16[64,4096]{1,0:T(8,128)(2,1)} %arrive.3.refs_0_, bf16[64,4096]{1,0:T(8,128)(2,1)} %copy-done.14, bf16[64,4096]{1,0:T(8,128)(2,1)} %copy-done.13, bf16[64,4096]{1,0:T(8,128)(2,1)} %copy-done.12, ...), custom_call_target="tpu_custom_call" | custom-call | flops 2415919104 | bytes 13631488 | tf_op jit(solution)/shard_map/expert/pallas_call | solution.py:242
  134.2 13.1 %collective-permute-done.13.refs_1_ = bf16[128,4096]{1,0:T(8,128)(2,1)S(1)} collective-permute-done((bf16[128,4096]{1,0:T(8,128)(2,1)}, bf16[128,4096]{1,0:T(8,128)(2,1)S(1)}, u32[]{:S(2)}, u32[]{:S(2)}) %collective-permute-start.13) | collective-permute-done | bytes 1048608 | tf_op jit(solution)/shard_map/ppermute | solution.py:311
  147.3 1.0 copy-done.3
  148.3 3.0 arrive.5.refs_0_
  151.3 3.1 collective-permute-start.19
  154.5 3.2 collective-permute-start.12
  157.7 17.0 %collective-permute-done.17.refs_3_ = bf16[128,4096]{1,0:T(8,128)(2,1)} collective-permute-done((bf16[128,4096]{1,0:T(8,128)(2,1)S(1)}, bf16[128,4096]{1,0:T(8,128)(2,1)}, u32[]{:S(2)}, u32[]{:S(2)}) %collective-permute-start.17) | collective-permute-done | bytes 1048608 | tf_op jit(solution)/shard_map/ppermute | solution.py:311
  174.7 13.2 %expert.4 = (bf16[128,4096]{1,0:T(8,128)(2,1)}, bf16[128,4096]{1,0:T(8,128)(2,1)}, bf16[128,4096]{1,0:T(8,128)(2,1)}, bf16[128,4096]{1,0:T(8,128)(2,1)}) custom-call(bf16[128,4096]{1,0:T(8,128)(2,1)} %arrive.4.refs_0_, bf16[128,4096]{1,0:T(8,128)(2,1)} %copy-done.27, bf16[128,4096]{1,0:T(8,128)(2,1)} %copy-done.28, ...), custom_call_target="tpu_custom_call" | custom-call | flops 4831838208 | bytes 17825792 | tf_op jit(solution)/shard_map/expert/pallas_call | solution.py:242
  188.0 0.1 add_convert_fusion.2
  188.1 2.1 collective-permute-start.15
  190.2 0.3 collective-permute-start.22
  190.4 3.1 collective-permute-start.23
  193.6 10.7 %collective-permute-done.15.last = bf16[64,4096]{1,0:T(8,128)(2,1)S(1)} collective-permute-done((bf16[64,4096]{1,0:T(8,128)(2,1)S(1)}, bf16[64,4096]{1,0:T(8,128)(2,1)S(1)}, u32[]{:S(2)}, u32[]{:S(2)}) %collective-permute-start.15) | collective-permute-done | bytes 524320 | tf_op jit(solution)/shard_map/ppermute | solution.py:311
  204.3 0.8 copy-done.17
  205.1 2.7 leave.3
  207.8 10.4 %all-to-all-start.2 = ((bf16[64,8,512]{2,1,0:T(8,128)(2,1)}), bf16[64,8,512]{2,1,0:T(8,128)(2,1)S(1)}, u32[]{:S(2)}, u32[]{:S(2)}) async-start(bf16[64,8,512]{2,1,0:T(8,128)(2,1)} %bitcast.38), calls=%async_computation.2 | async-start | bytes 1048576 | tf_op jit(solution)/shard_map/all_to_all | solution.py:320
  218.1 0.9 collective-permute-start.18
  219.0 0.2 add_convert_fusion.1
  219.2 2.5 collective-permute-start.21
  221.8 0.5 collective-permute-done.22.refs_2_
  222.3 14.5 %collective-permute-done.23.refs_3_ = bf16[128,4096]{1,0:T(8,128)(2,1)} collective-permute-done((bf16[128,4096]{1,0:T(8,128)(2,1)}, bf16[128,4096]{1,0:T(8,128)(2,1)}, u32[]{:S(2)}, u32[]{:S(2)}) %collective-permute-start.23) | collective-permute-done | bytes 1048608 | tf_op jit(solution)/shard_map/ppermute | solution.py:307
  236.8 13.2 %expert.5 = (bf16[128,4096]{1,0:T(8,128)(2,1)}, bf16[128,4096]{1,0:T(8,128)(2,1)}, bf16[128,4096]{1,0:T(8,128)(2,1)}, bf16[128,4096]{1,0:T(8,128)(2,1)}) custom-call(bf16[128,4096]{1,0:T(8,128)(2,1)} %arrive.5.refs_0_, bf16[128,4096]{1,0:T(8,128)(2,1)} %collective-permute-done.19.refs_1_, bf16[128,4096]{1,0:T(8,128)(2,1)} %collective-permute-done.22.refs_2_, ...), custom_call_target="tpu_custom_call" | custom-call | flops 4831838208 | bytes 17825792 | tf_op jit(solution)/shard_map/expert/pallas_call | solution.py:242
  250.0 4.8 %collective-permute-done.21.last = bf16[128,4096]{1,0:T(8,128)(2,1)S(1)} collective-permute-done((bf16[128,4096]{1,0:T(8,128)(2,1)S(1)}, bf16[128,4096]{1,0:T(8,128)(2,1)S(1)}, u32[]{:S(2)}, u32[]{:S(2)}) %collective-permute-start.21) | collective-permute-done | bytes 1048608 | tf_op jit(solution)/shard_map/ppermute | solution.py:307
  254.8 1.0 copy-done.8
  255.8 3.8 %leave.4 = bf16[512,1024]{1,0:T(8,128)(2,1)} custom-call(bf16[128,4096]{1,0:T(8,128)(2,1)} %get-tuple-element.38.own, bf16[128,4096]{1,0:T(8,128)(2,1)} %copy-done.7, bf16[128,4096]{1,0:T(8,128)(2,1)} %copy-done.8), custom_call_target="tpu_custom_call" | custom-call | tf_op jit(solution)/shard_map/leave/pallas_call | solution.py:192
  259.6 10.6 %all-to-all-start.4 = ((bf16[64,8,1024]{2,1,0:T(8,128)(2,1)}), bf16[64,8,1024]{2,1,0:T(8,128)(2,1)S(1)}, u32[]{:S(2)}, u32[]{:S(2)}) async-start(bf16[64,8,1024]{2,1,0:T(8,128)(2,1)} %bitcast.25), calls=%async_computation.4 | async-start | bytes 2097152 | tf_op jit(solution)/shard_map/all_to_all | solution.py:320
  270.2 3.8 %collective-permute-start.24 = (bf16[128,4096]{1,0:T(8,128)(2,1)}, bf16[128,4096]{1,0:T(8,128)(2,1)S(1)}, u32[]{:S(2)}, u32[]{:S(2)}) collective-permute-start(bf16[128,4096]{1,0:T(8,128)(2,1)} %get-tuple-element.50), channel_id=1, source_target_pairs={{0,1},{1,2},{2,3},{3,0},{4,5},{5,6},{6,7},{7,4},{8,9},{9,10},{10,1... | collective-permute-start | bytes 3145736 | tf_op jit(solution)/shard_map/ppermute | solution.py:307
  274.0 1.5 add_convert_fusion
  275.6 21.4 %collective-permute-done.24.other = bf16[128,4096]{1,0:T(8,128)(2,1)S(1)} collective-permute-done((bf16[128,4096]{1,0:T(8,128)(2,1)}, bf16[128,4096]{1,0:T(8,128)(2,1)S(1)}, u32[]{:S(2)}, u32[]{:S(2)}) %collective-permute-start.24) | collective-permute-done | bytes 1048608 | tf_op jit(solution)/shard_map/ppermute | solution.py:307
  296.9 4.7 %collective-permute-done.26.last = bf16[128,4096]{1,0:T(8,128)(2,1)S(1)} collective-permute-done((bf16[128,4096]{1,0:T(8,128)(2,1)S(1)}, bf16[128,4096]{1,0:T(8,128)(2,1)S(1)}, u32[]{:S(2)}, u32[]{:S(2)}) %collective-permute-start.26) | collective-permute-done | bytes 1048608 | tf_op jit(solution)/shard_map/ppermute | solution.py:311
  301.6 1.0 copy-done.10
  302.6 3.7 %leave.5 = bf16[512,1024]{1,0:T(8,128)(2,1)} custom-call(bf16[128,4096]{1,0:T(8,128)(2,1)} %get-tuple-element.49.own, bf16[128,4096]{1,0:T(8,128)(2,1)} %copy-done.9, bf16[128,4096]{1,0:T(8,128)(2,1)} %copy-done.10), custom_call_target="tpu_custom_call" | custom-call | tf_op jit(solution)/shard_map/leave/pallas_call | solution.py:192
  306.3 39.4 %all_to_all.31 = bf16[64,8,1024]{2,1,0:T(8,128)(2,1)} all-to-all(bf16[64,8,1024]{2,1,0:T(8,128)(2,1)} %bitcast.26), channel_id=1, replica_groups=mesh['ep'=64,'sp'=4] {'ep'}, dimensions={0} | all-to-all | bytes 2097152 | tf_op jit(solution)/shard_map/all_to_all | solution.py:320
  345.7 5.3 %combine.1 = bf16[128,4096]{1,0:T(8,128)(2,1)} custom-call(s32[1]{0:T(128)} %bitcast.sp_ref, s32[2,512]{1,0:T(2,128)} %bitcast.42, s32[2,128]{1,0:T(2,128)} %bitcast.43, bf16[512,512]{1,0:T(8,128)(2,1)} %bitcast.36, bf16[512,1024]{1,0:T(8,128)(2,1)} %bitcast.21, bf16[512,1024]{1,0:T(8,128)(2,1)} %bitcast.22), custom_call_target="tpu_custom_call" | custom-call | tf_op jit(solution)/shard_map/combine/pallas_call | solution.py:295
  (82 shorter events, 0.5 us)
Async XLA Ops:
  0.6 3.0 copy-start
  0.6 15.5 %collective-permute-start = (bf16[128,1024]{1,0:T(8,128)(2,1)}, bf16[128,1024]{1,0:T(8,128)(2,1)S(1)}, u32[]{:S(2)}, u32[]{:S(2)}) collective-permute-start(bf16[128,1024]{1,0:T(8,128)(2,1)} %refs_0_.1), channel_id=1, source_target_pairs={{0,1},{1,2},{2,3},{3,0},{4,5},{5,6},{6,7},{7,4},{8,9},{9,10},{10,1... | collective-permute-start | bytes 786440 | tf_op jit(solution)/shard_map/ppermute | solution.py:307
  2.9 13.5 %collective-permute-start.4 = (bf16[128,1024]{1,0:T(8,128)(2,1)}, bf16[128,1024]{1,0:T(8,128)(2,1)S(1)}, u32[]{:S(2)}, u32[]{:S(2)}) collective-permute-start(bf16[128,1024]{1,0:T(8,128)(2,1)} %refs_4_.1), channel_id=1, source_target_pairs={{0,3},{1,0},{2,1},{3,2},{4,7},{5,4},{6,5},{7,6},{8,11},{9,8},{10,9... | collective-permute-start | bytes 786440 | tf_op jit(solution)/shard_map/ppermute | solution.py:311
  5.0 22.8 %copy-start.15 = (bf16[64,1024]{1,0:T(8,128)(2,1)}, bf16[64,1024]{1,0:T(8,128)(2,1)S(1)}, u32[]{:S(2)}) copy-start(bf16[64,1024]{1,0:T(8,128)(2,1)S(1)} %pad_maximum_fusion.refs_8_) | copy-start | bytes 393220
  5.1 11.0 %collective-permute-start.7 = (bf16[64,1024]{1,0:T(8,128)(2,1)S(1)}, bf16[64,1024]{1,0:T(8,128)(2,1)S(1)}, u32[]{:S(2)}, u32[]{:S(2)}) collective-permute-start(bf16[64,1024]{1,0:T(8,128)(2,1)S(1)} %pad_maximum_fusion.refs_8_), channel_id=1, source_target_pairs={{0,3},{1,0},{2,1},{3,2},{4,7},{5,4},{6,5},{7,6},{8,11},{9,8},{10,9... | collective-permute-start | bytes 393224 | tf_op jit(solution)/shard_map/ppermute | solution.py:311
  5.8 12.5 %collective-permute-start.6 = (bf16[64,1024]{1,0:T(8,128)(2,1)S(1)}, bf16[64,1024]{1,0:T(8,128)(2,1)S(1)}, u32[]{:S(2)}, u32[]{:S(2)}) collective-permute-start(bf16[64,1024]{1,0:T(8,128)(2,1)S(1)} %pad_maximum_fusion.refs_8_), channel_id=1, source_target_pairs={{0,1},{1,2},{2,3},{3,0},{4,5},{5,6},{6,7},{7,4},{8,9},{9,10},{10,1... | collective-permute-start | bytes 393224 | tf_op jit(solution)/shard_map/ppermute | solution.py:307
  8.5 19.3 %collective-permute-start.1 = (bf16[128,1024]{1,0:T(8,128)(2,1)}, bf16[128,1024]{1,0:T(8,128)(2,1)S(1)}, u32[]{:S(2)}, u32[]{:S(2)}) collective-permute-start(bf16[128,1024]{1,0:T(8,128)(2,1)} %refs_0_.1), channel_id=1, source_target_pairs={{0,3},{1,0},{2,1},{3,2},{4,7},{5,4},{6,5},{7,6},{8,11},{9,8},{10,9... | collective-permute-start | bytes 786440 | tf_op jit(solution)/shard_map/ppermute | solution.py:311
  16.1 11.8 %copy-start.24 = (bf16[64,1024]{1,0:T(8,128)(2,1)}, bf16[64,1024]{1,0:T(8,128)(2,1)S(1)}, u32[]{:S(2)}) copy-start(bf16[64,1024]{1,0:T(8,128)(2,1)S(1)} %collective-permute-done.7.refs_10_) | copy-start | bytes 393220
  16.1 11.7 %collective-permute-start.3 = (bf16[128,1024]{1,0:T(8,128)(2,1)}, bf16[128,1024]{1,0:T(8,128)(2,1)S(1)}, u32[]{:S(2)}, u32[]{:S(2)}) collective-permute-start(bf16[128,1024]{1,0:T(8,128)(2,1)} %refs_4_.1), channel_id=1, source_target_pairs={{0,1},{1,2},{2,3},{3,0},{4,5},{5,6},{6,7},{7,4},{8,9},{9,10},{10,1... | collective-permute-start | bytes 786440 | tf_op jit(solution)/shard_map/ppermute | solution.py:307
  16.1 11.8 %copy-start.18 = (bf16[128,1024]{1,0:T(8,128)(2,1)}, bf16[128,1024]{1,0:T(8,128)(2,1)S(1)}, u32[]{:S(2)}) copy-start(bf16[128,1024]{1,0:T(8,128)(2,1)S(1)} %collective-permute-done.refs_1_) | copy-start | bytes 786436
  16.1 11.7 %collective-permute-start.2 = (bf16[128,1024]{1,0:T(8,128)(2,1)S(1)}, bf16[128,1024]{1,0:T(8,128)(2,1)S(1)}, u32[]{:S(2)}, u32[]{:S(2)}) collective-permute-start(bf16[128,1024]{1,0:T(8,128)(2,1)S(1)} %collective-permute-done.refs_1_), channel_id=1, source_target_pairs={{0,1},{1,2},{2,3},{3,0},{4,5},{5,6},{6,7},{7,4},{8,9},{9,10},{10,1... | collective-permute-start | bytes 786440 | tf_op jit(solution)/shard_map/ppermute | solution.py:307
  16.4 11.4 %copy-start.19 = (bf16[128,1024]{1,0:T(8,128)(2,1)}, bf16[128,1024]{1,0:T(8,128)(2,1)S(1)}, u32[]{:S(2)}) copy-start(bf16[128,1024]{1,0:T(8,128)(2,1)S(1)} %collective-permute-done.4.refs_6_) | copy-start | bytes 786436
  16.4 11.4 %collective-permute-start.5 = (bf16[128,1024]{1,0:T(8,128)(2,1)S(1)}, bf16[128,1024]{1,0:T(8,128)(2,1)S(1)}, u32[]{:S(2)}, u32[]{:S(2)}) collective-permute-start(bf16[128,1024]{1,0:T(8,128)(2,1)S(1)} %collective-permute-done.4.refs_6_), channel_id=1, source_target_pairs={{0,3},{1,0},{2,1},{3,2},{4,7},{5,4},{6,5},{7,6},{8,11},{9,8},{10,9... | collective-permute-start | bytes 786440 | tf_op jit(solution)/shard_map/ppermute | solution.py:311
  18.2 9.7 %copy-start.25 = (bf16[64,1024]{1,0:T(8,128)(2,1)}, bf16[64,1024]{1,0:T(8,128)(2,1)S(1)}, u32[]{:S(2)}) copy-start(bf16[64,1024]{1,0:T(8,128)(2,1)S(1)} %collective-permute-done.6.refs_9_) | copy-start | bytes 393220
  18.2 9.6 %collective-permute-start.8 = (bf16[64,1024]{1,0:T(8,128)(2,1)S(1)}, bf16[64,1024]{1,0:T(8,128)(2,1)S(1)}, u32[]{:S(2)}, u32[]{:S(2)}) collective-permute-start(bf16[64,1024]{1,0:T(8,128)(2,1)S(1)} %collective-permute-done.6.refs_9_), channel_id=1, source_target_pairs={{0,1},{1,2},{2,3},{3,0},{4,5},{5,6},{6,7},{7,4},{8,9},{9,10},{10,1... | collective-permute-start | bytes 393224 | tf_op jit(solution)/shard_map/ppermute | solution.py:307
  27.8 0.7 copy-start.26
  27.8 0.8 copy-start.20
  27.8 0.8 copy-start.21
  27.8 0.9 copy-start.22
  27.9 1.0 copy-start.23
  71.6 34.9 %all-to-all-start.1 = ((bf16[64,8,1024]{2,1,0:T(8,128)(2,1)}), bf16[64,8,1024]{2,1,0:T(8,128)(2,1)S(1)}, u32[]{:S(2)}, u32[]{:S(2)}) async-start(bf16[64,8,1024]{2,1,0:T(8,128)(2,1)} %bitcast.39), calls=%async_computation.1 | async-start | bytes 2097152 | tf_op jit(solution)/shard_map/all_to_all | solution.py:320
  79.7 16.5 %collective-permute-start.11 = (bf16[64,4096]{1,0:T(8,128)(2,1)}, bf16[64,4096]{1,0:T(8,128)(2,1)S(1)}, u32[]{:S(2)}, u32[]{:S(2)}) collective-permute-start(bf16[64,4096]{1,0:T(8,128)(2,1)} %arrive.3.refs_0_), channel_id=1, source_target_pairs={{0,2},{1,3},{2,0},{3,1},{4,6},{5,7},{6,4},{7,5},{8,10},{9,11},{10,... | collective-permute-start | bytes 1572872 | tf_op jit(solution)/shard_map/ppermute | solution.py:315
  80.9 25.6 %collective-permute-start.10 = (bf16[64,4096]{1,0:T(8,128)(2,1)}, bf16[64,4096]{1,0:T(8,128)(2,1)S(1)}, u32[]{:S(2)}, u32[]{:S(2)}) collective-permute-start(bf16[64,4096]{1,0:T(8,128)(2,1)} %arrive.3.refs_0_), channel_id=1, source_target_pairs={{0,3},{1,0},{2,1},{3,2},{4,7},{5,4},{6,5},{7,6},{8,11},{9,8},{10,9... | collective-permute-start | bytes 1572872 | tf_op jit(solution)/shard_map/ppermute | solution.py:311
  82.0 24.5 %collective-permute-start.9 = (bf16[64,4096]{1,0:T(8,128)(2,1)}, bf16[64,4096]{1,0:T(8,128)(2,1)S(1)}, u32[]{:S(2)}, u32[]{:S(2)}) collective-permute-start(bf16[64,4096]{1,0:T(8,128)(2,1)} %arrive.3.refs_0_), channel_id=1, source_target_pairs={{0,1},{1,2},{2,3},{3,0},{4,5},{5,6},{6,7},{7,4},{8,9},{9,10},{10,1... | collective-permute-start | bytes 1572872 | tf_op jit(solution)/shard_map/ppermute | solution.py:307
  96.2 24.5 %copy-start.12 = (bf16[64,4096]{1,0:T(8,128)(2,1)}, bf16[64,4096]{1,0:T(8,128)(2,1)S(1)}, u32[]{:S(2)}) copy-start(bf16[64,4096]{1,0:T(8,128)(2,1)S(1)} %collective-permute-done.11.refs_3_) | copy-start | bytes 1572868
  106.5 14.2 %copy-start.13 = (bf16[64,4096]{1,0:T(8,128)(2,1)}, bf16[64,4096]{1,0:T(8,128)(2,1)S(1)}, u32[]{:S(2)}) copy-start(bf16[64,4096]{1,0:T(8,128)(2,1)S(1)} %collective-permute-done.10.refs_2_) | copy-start | bytes 1572868
  106.5 0.8 copy-start.14
  106.5 11.2 %copy-start.2 = (bf16[64,8,1024]{2,1,0:T(8,128)(2,1)}, bf16[64,8,1024]{2,1,0:T(8,128)(2,1)S(1)}, u32[]{:S(2)}) copy-start(bf16[64,8,1024]{2,1,0:T(8,128)(2,1)S(1)} %all-to-all-done.1) | copy-start | bytes 3145732
  107.4 39.9 %all-to-all-start.3 = ((bf16[64,8,1024]{2,1,0:T(8,128)(2,1)}), bf16[64,8,1024]{2,1,0:T(8,128)(2,1)S(1)}, u32[]{:S(2)}, u32[]{:S(2)}) async-start(bf16[64,8,1024]{2,1,0:T(8,128)(2,1)} %bitcast.13), calls=%async_computation.3 | async-start | bytes 2097152 | tf_op jit(solution)/shard_map/all_to_all | solution.py:320
  120.7 26.5 %collective-permute-start.13 = (bf16[128,4096]{1,0:T(8,128)(2,1)}, bf16[128,4096]{1,0:T(8,128)(2,1)S(1)}, u32[]{:S(2)}, u32[]{:S(2)}) collective-permute-start(bf16[128,4096]{1,0:T(8,128)(2,1)} %arrive.4.refs_0_), channel_id=1, source_target_pairs={{0,3},{1,0},{2,1},{3,2},{4,7},{5,4},{6,5},{7,6},{8,11},{9,8},{10,9... | collective-permute-start | bytes 3145736 | tf_op jit(solution)/shard_map/ppermute | solution.py:311
  121.0 30.3 %collective-permute-start.16 = (bf16[128,4096]{1,0:T(8,128)(2,1)}, bf16[128,4096]{1,0:T(8,128)(2,1)S(1)}, u32[]{:S(2)}, u32[]{:S(2)}) collective-permute-start(bf16[128,4096]{1,0:T(8,128)(2,1)} %arrive.4.refs_0_), channel_id=1, source_target_pairs={{0,1},{1,2},{2,3},{3,0},{4,5},{5,6},{6,7},{7,4},{8,9},{9,10},{10,1... | collective-permute-start | bytes 3145736 | tf_op jit(solution)/shard_map/ppermute | solution.py:307
  147.3 27.4 %copy-start.27 = (bf16[128,4096]{1,0:T(8,128)(2,1)}, bf16[128,4096]{1,0:T(8,128)(2,1)S(1)}, u32[]{:S(2)}) copy-start(bf16[128,4096]{1,0:T(8,128)(2,1)S(1)} %collective-permute-done.13.refs_1_) | copy-start | bytes 3145732
  147.3 27.4 %collective-permute-start.17 = (bf16[128,4096]{1,0:T(8,128)(2,1)S(1)}, bf16[128,4096]{1,0:T(8,128)(2,1)}, u32[]{:S(2)}, u32[]{:S(2)}) collective-permute-start(bf16[128,4096]{1,0:T(8,128)(2,1)S(1)} %collective-permute-done.13.refs_1_), channel_id=1, source_target_pairs={{0,3},{1,0},{2,1},{3,2},{4,7},{5,4},{6,5},{7,6},{8,11},{9,8},{10,9... | collective-permute-start | bytes 3145736 | tf_op jit(solution)/shard_map/ppermute | solution.py:311
  147.3 1.0 copy-start.3
  147.3 7.2 %copy-start.30 = (bf16[64,4096]{1,0:T(8,128)(2,1)S(1)}, bf16[64,4096]{1,0:T(8,128)(2,1)}, u32[]{:S(2)}) copy-start(bf16[64,4096]{1,0:T(8,128)(2,1)} %get-tuple-element.36) | copy-start | bytes 1572868
  147.3 7.2 %copy-start.29 = (bf16[64,4096]{1,0:T(8,128)(2,1)S(1)}, bf16[64,4096]{1,0:T(8,128)(2,1)}, u32[]{:S(2)}) copy-start(bf16[64,4096]{1,0:T(8,128)(2,1)} %get-tuple-element.31) | copy-start | bytes 1572868
  151.3 23.4 %copy-start.28 = (bf16[128,4096]{1,0:T(8,128)(2,1)}, bf16[128,4096]{1,0:T(8,128)(2,1)S(1)}, u32[]{:S(2)}) copy-start(bf16[128,4096]{1,0:T(8,128)(2,1)S(1)} %collective-permute-done.16.refs_2_) | copy-start | bytes 3145732
  151.3 36.5 %collective-permute-start.19 = (bf16[128,4096]{1,0:T(8,128)(2,1)}, bf16[128,4096]{1,0:T(8,128)(2,1)}, u32[]{:S(2)}, u32[]{:S(2)}) collective-permute-start(bf16[128,4096]{1,0:T(8,128)(2,1)} %arrive.5.refs_0_), channel_id=1, source_target_pairs={{0,1},{1,2},{2,3},{3,0},{4,5},{5,6},{6,7},{7,4},{8,9},{9,10},{10,1... | collective-permute-start | bytes 3145736 | tf_op jit(solution)/shard_map/ppermute | solution.py:307
  154.5 33.5 %collective-permute-start.14 = (bf16[64,4096]{1,0:T(8,128)(2,1)S(1)}, bf16[64,4096]{1,0:T(8,128)(2,1)S(1)}, u32[]{:S(2)}, u32[]{:S(2)}) collective-permute-start(bf16[64,4096]{1,0:T(8,128)(2,1)S(1)} %copy-done.30), channel_id=1, source_target_pairs={{0,3},{1,0},{2,1},{3,2},{4,7},{5,4},{6,5},{7,6},{8,11},{9,8},{10,9... | collective-permute-start | bytes 1572872 | tf_op jit(solution)/shard_map/ppermute | solution.py:311
  154.5 33.5 %copy-start.11 = (bf16[64,4096]{1,0:T(8,128)(2,1)S(1)}, bf16[64,4096]{1,0:T(8,128)(2,1)}, u32[]{:S(2)}) copy-start(bf16[64,4096]{1,0:T(8,128)(2,1)} %get-tuple-element.32) | copy-start | bytes 1572868
  154.5 39.1 %collective-permute-start.12 = (bf16[64,4096]{1,0:T(8,128)(2,1)S(1)}, bf16[64,4096]{1,0:T(8,128)(2,1)S(1)}, u32[]{:S(2)}, u32[]{:S(2)}) collective-permute-start(bf16[64,4096]{1,0:T(8,128)(2,1)S(1)} %copy-done.29), channel_id=1, source_target_pairs={{0,1},{1,2},{2,3},{3,0},{4,5},{5,6},{6,7},{7,4},{8,9},{9,10},{10,1... | collective-permute-start | bytes 1572872 | tf_op jit(solution)/shard_map/ppermute | solution.py:307
  187.9 31.1 %collective-permute-start.20 = (bf16[128,4096]{1,0:T(8,128)(2,1)}, bf16[128,4096]{1,0:T(8,128)(2,1)S(1)}, u32[]{:S(2)}, u32[]{:S(2)}) collective-permute-start(bf16[128,4096]{1,0:T(8,128)(2,1)} %get-tuple-element.46), channel_id=1, source_target_pairs={{0,1},{1,2},{2,3},{3,0},{4,5},{5,6},{6,7},{7,4},{8,9},{9,10},{10,1... | collective-permute-start | bytes 3145736 | tf_op jit(solution)/shard_map/ppermute | solution.py:307
  188.0 31.0 %copy-start.5 = (bf16[128,4096]{1,0:T(8,128)(2,1)S(1)}, bf16[128,4096]{1,0:T(8,128)(2,1)}, u32[]{:S(2)}) copy-start(bf16[128,4096]{1,0:T(8,128)(2,1)} %get-tuple-element.40) | copy-start | bytes 3145732
  188.1 16.2 %collective-permute-start.15 = (bf16[64,4096]{1,0:T(8,128)(2,1)S(1)}, bf16[64,4096]{1,0:T(8,128)(2,1)S(1)}, u32[]{:S(2)}, u32[]{:S(2)}) collective-permute-start(bf16[64,4096]{1,0:T(8,128)(2,1)S(1)} %add_convert_fusion.2), channel_id=1, source_target_pairs={{0,3},{1,0},{2,1},{3,2},{4,7},{5,4},{6,5},{7,6},{8,11},{9,8},{10,9... | collective-permute-start | bytes 1572872 | tf_op jit(solution)/shard_map/ppermute | solution.py:311
  190.2 32.1 %collective-permute-start.22 = (bf16[128,4096]{1,0:T(8,128)(2,1)}, bf16[128,4096]{1,0:T(8,128)(2,1)}, u32[]{:S(2)}, u32[]{:S(2)}) collective-permute-start(bf16[128,4096]{1,0:T(8,128)(2,1)} %arrive.5.refs_0_), channel_id=1, source_target_pairs={{0,3},{1,0},{2,1},{3,2},{4,7},{5,4},{6,5},{7,6},{8,11},{9,8},{10,9... | collective-permute-start | bytes 3145736 | tf_op jit(solution)/shard_map/ppermute | solution.py:311
  190.4 46.4 %collective-permute-start.23 = (bf16[128,4096]{1,0:T(8,128)(2,1)}, bf16[128,4096]{1,0:T(8,128)(2,1)}, u32[]{:S(2)}, u32[]{:S(2)}) collective-permute-start(bf16[128,4096]{1,0:T(8,128)(2,1)} %collective-permute-done.19.refs_1_), channel_id=1, source_target_pairs={{0,1},{1,2},{2,3},{3,0},{4,5},{5,6},{6,7},{7,4},{8,9},{9,10},{10,1... | collective-permute-start | bytes 3145736 | tf_op jit(solution)/shard_map/ppermute | solution.py:307
  193.6 10.7 %copy-start.16 = (bf16[64,4096]{1,0:T(8,128)(2,1)}, bf16[64,4096]{1,0:T(8,128)(2,1)S(1)}, u32[]{:S(2)}) copy-start(bf16[64,4096]{1,0:T(8,128)(2,1)S(1)} %collective-permute-done.12.other) | copy-start | bytes 1572868
  204.3 0.8 copy-start.17
  207.8 51.8 %all-to-all-start.2 = ((bf16[64,8,512]{2,1,0:T(8,128)(2,1)}), bf16[64,8,512]{2,1,0:T(8,128)(2,1)S(1)}, u32[]{:S(2)}, u32[]{:S(2)}) async-start(bf16[64,8,512]{2,1,0:T(8,128)(2,1)} %bitcast.38), calls=%async_computation.2 | async-start | bytes 1048576 | tf_op jit(solution)/shard_map/all_to_all | solution.py:320
  218.1 31.9 %collective-permute-start.18 = (bf16[128,4096]{1,0:T(8,128)(2,1)}, bf16[128,4096]{1,0:T(8,128)(2,1)S(1)}, u32[]{:S(2)}, u32[]{:S(2)}) collective-permute-start(bf16[128,4096]{1,0:T(8,128)(2,1)} %get-tuple-element.39), channel_id=1, source_target_pairs={{0,3},{1,0},{2,1},{3,2},{4,7},{5,4},{6,5},{7,6},{8,11},{9,8},{10,9... | collective-permute-start | bytes 3145736 | tf_op jit(solution)/shard_map/ppermute | solution.py:311
  219.2 35.6 %collective-permute-start.21 = (bf16[128,4096]{1,0:T(8,128)(2,1)S(1)}, bf16[128,4096]{1,0:T(8,128)(2,1)S(1)}, u32[]{:S(2)}, u32[]{:S(2)}) collective-permute-start(bf16[128,4096]{1,0:T(8,128)(2,1)S(1)} %add_convert_fusion.1), channel_id=1, source_target_pairs={{0,1},{1,2},{2,3},{3,0},{4,5},{5,6},{6,7},{7,4},{8,9},{9,10},{10,1... | collective-permute-start | bytes 3145736 | tf_op jit(solution)/shard_map/ppermute | solution.py:307
  250.0 24.0 %collective-permute-start.25 = (bf16[128,4096]{1,0:T(8,128)(2,1)}, bf16[128,4096]{1,0:T(8,128)(2,1)}, u32[]{:S(2)}, u32[]{:S(2)}) collective-permute-start(bf16[128,4096]{1,0:T(8,128)(2,1)} %get-tuple-element.52), channel_id=1, source_target_pairs={{0,3},{1,0},{2,1},{3,2},{4,7},{5,4},{6,5},{7,6},{8,11},{9,8},{10,9... | collective-permute-start | bytes 3145736 | tf_op jit(solution)/shard_map/ppermute | solution.py:311
  250.0 4.8 %copy-start.7 = (bf16[128,4096]{1,0:T(8,128)(2,1)}, bf16[128,4096]{1,0:T(8,128)(2,1)S(1)}, u32[]{:S(2)}) copy-start(bf16[128,4096]{1,0:T(8,128)(2,1)S(1)} %collective-permute-done.18.other) | copy-start | bytes 3145732
  254.8 1.0 copy-start.8
  259.6 14.4 %copy-start.6 = (bf16[128,4096]{1,0:T(8,128)(2,1)S(1)}, bf16[128,4096]{1,0:T(8,128)(2,1)}, u32[]{:S(2)}) copy-start(bf16[128,4096]{1,0:T(8,128)(2,1)} %get-tuple-element.51) | copy-start | bytes 3145732
  259.6 15.9 %copy-start.4 = (bf16[64,8,512]{2,1,0:T(8,128)(2,1)}, bf16[64,8,512]{2,1,0:T(8,128)(2,1)S(1)}, u32[]{:S(2)}) copy-start(bf16[64,8,512]{2,1,0:T(8,128)(2,1)S(1)} %all-to-all-done.2) | copy-start | bytes 1572868
  259.6 46.7 %all-to-all-start.4 = ((bf16[64,8,1024]{2,1,0:T(8,128)(2,1)}), bf16[64,8,1024]{2,1,0:T(8,128)(2,1)S(1)}, u32[]{:S(2)}, u32[]{:S(2)}) async-start(bf16[64,8,1024]{2,1,0:T(8,128)(2,1)} %bitcast.25), calls=%async_computation.4 | async-start | bytes 2097152 | tf_op jit(solution)/shard_map/all_to_all | solution.py:320
  270.2 26.7 %collective-permute-start.24 = (bf16[128,4096]{1,0:T(8,128)(2,1)}, bf16[128,4096]{1,0:T(8,128)(2,1)S(1)}, u32[]{:S(2)}, u32[]{:S(2)}) collective-permute-start(bf16[128,4096]{1,0:T(8,128)(2,1)} %get-tuple-element.50), channel_id=1, source_target_pairs={{0,1},{1,2},{2,3},{3,0},{4,5},{5,6},{6,7},{7,4},{8,9},{9,10},{10,1... | collective-permute-start | bytes 3145736 | tf_op jit(solution)/shard_map/ppermute | solution.py:307
  275.5 26.1 %collective-permute-start.26 = (bf16[128,4096]{1,0:T(8,128)(2,1)S(1)}, bf16[128,4096]{1,0:T(8,128)(2,1)S(1)}, u32[]{:S(2)}, u32[]{:S(2)}) collective-permute-start(bf16[128,4096]{1,0:T(8,128)(2,1)S(1)} %add_convert_fusion), channel_id=1, source_target_pairs={{0,3},{1,0},{2,1},{3,2},{4,7},{5,4},{6,5},{7,6},{8,11},{9,8},{10,9... | collective-permute-start | bytes 3145736 | tf_op jit(solution)/shard_map/ppermute | solution.py:311
  296.9 4.7 %copy-start.9 = (bf16[128,4096]{1,0:T(8,128)(2,1)}, bf16[128,4096]{1,0:T(8,128)(2,1)S(1)}, u32[]{:S(2)}) copy-start(bf16[128,4096]{1,0:T(8,128)(2,1)S(1)} %collective-permute-done.24.other) | copy-start | bytes 3145732
  301.6 1.0 copy-start.10
  306.3 39.4 %copy-start.1 = (bf16[64,8,1024]{2,1,0:T(8,128)(2,1)}, bf16[64,8,1024]{2,1,0:T(8,128)(2,1)S(1)}, u32[]{:S(2)}) copy-start(bf16[64,8,1024]{2,1,0:T(8,128)(2,1)S(1)} %all-to-all-done.4) | copy-start | bytes 3145732

commit v3 on v2

--- a/solution.py
+++ b/solution.py
@@ -200,7 +200,7 @@
     )(*terms)
 
 
-STEPS = 4
+STEPS = 2
 
 
 def expert_kernel(n, *refs):

time: 358 us -> 358 us (level)
  Pallas kernels: 72.3 us -> 68.7 us
    pallas_call x3, Pallas kernels: 36.6 us -> 33 us  [expert(): pl.pallas_call(functools.partial(expert_kernel, n), out_shape=[jax.ShapeD...]
  transfers between devices with their start and end apart: 31 -> 31, of which waited for: 12 -> 12; matrix products, arithmetic and copies ran while one was open for 2% -> 2% of each run, Pallas kernels for 16% -> 15%
where the time goes in v3:
time: 358 us; the launch traced here: 351 us
  waiting for transfers between devices  125 us (35%)
  starting transfers between devices  74 us (21%)
  blocking collectives  70.1 us (20%)
  Pallas kernels  68.7 us (19%)
  local copies, waits for them, and re-layouts  8.18 us (2%)
    all_to_all x2, blocking collectives, exchange(): moved = lax.all_to_all(cut, 'ep', split_axis=0, concat_axis=0, tiled=True)  70.1 us
    ppermute x13, waiting for transfers between devices, left(): return lax.ppermute(x, 'sp', [(i, (i + 3) % 4) for i in range(4)])  65.6 us
    ppermute x13, waiting for transfers between devices, right(): return lax.ppermute(x, 'sp', [(i, (i + 1) % 4) for i in range(4)])  47.9 us
    all_to_all x4, starting transfers between devices, exchange(): moved = lax.all_to_all(cut, 'ep', split_axis=0, concat_axis=0, tiled=True)  37.2 us
    pallas_call x3, Pallas kernels, expert(): pl.pallas_call(functools.partial(expert_kernel, n), out_shape=[jax.ShapeD...  33 us
    ppermute x13, starting transfers between devices, right(): return lax.ppermute(x, 'sp', [(i, (i + 1) % 4) for i in range(4)])  28.6 us
    pallas_call x1, Pallas kernels, attention(): pl.pallas_call(attention_kernel, out_shape=outs, in_specs=[SMEM_SPEC] * 2...  12 us
    ppermute x1, waiting for transfers between devices, across(): return lax.ppermute(x, 'sp', [(i, (i + 2) % 4) for i in range(4)])  11.7 us
  transfers between devices with their start and end apart: 31, of which 12 were waited for; matrix products, arithmetic and copies ran while one was open for 2% of the time, Pallas kernels for 15%

profile of v3, /device:TPU:6, one launch (start us, length us, event | category | flops | bytes accessed | tf_op | source)
XLA Modules:
  0.0 351.5 jit_solution(711374847751099654)
XLA Ops:
  0.6 2.3 collective-permute-start
  3.6 0.2 convolution_convert_fusion.1
  3.8 1.2 convolution_convert_fusion
  5.1 0.7 collective-permute-start.7
  5.8 2.7 collective-permute-start.6
  8.5 7.6 %collective-permute-done.7.refs_10_ = bf16[64,1024]{1,0:T(8,128)(2,1)S(1)} collective-permute-done((bf16[64,1024]{1,0:T(8,128)(2,1)S(1)}, bf16[64,1024]{1,0:T(8,128)(2,1)S(1)}, u32[]{:S(2)}, u32[]{:S(2)}) %collective-permute-start.7) | collective-permute-done | bytes 131104 | tf_op jit(solution)/shard_map/ppermute | solution.py:311
  16.1 0.3 collective-permute-start.2
  16.4 1.8 collective-permute-start.5
  18.2 1.6 collective-permute-start.8
  19.8 1.3 reshape.56.refs_12_
  21.2 1.3 reshape.57.refs_13_
  22.5 5.3 %collective-permute-done.8.refs_11_ = bf16[64,1024]{1,0:T(8,128)(2,1)S(1)} collective-permute-done((bf16[64,1024]{1,0:T(8,128)(2,1)S(1)}, bf16[64,1024]{1,0:T(8,128)(2,1)S(1)}, u32[]{:S(2)}, u32[]{:S(2)}) %collective-permute-start.8) | collective-permute-done | bytes 131104 | tf_op jit(solution)/shard_map/ppermute | solution.py:307
  27.9 0.5 copy-done.26
  28.5 0.1 copy-done.20
  28.6 0.1 copy-done.22
  28.7 0.1 copy-done.23
  28.8 12.0 %attention.1 = (bf16[128,4096]{1,0:T(8,128)(2,1)}, bf16[512,512]{1,0:T(8,128)(2,1)}, bf16[512,1024]{1,0:T(8,128)(2,1)}, bf16[512,1024]{1,0:T(8,128)(2,1)}) custom-call(s32[1]{0:T(128)S(6)} %copy.16.user_ref, s32[1]{0:T(128)} %bitcast.sp_ref, bf16[128,4096]{1,0:T(8,128)(2,1)} %stream.1, bf16[128,4096]{1,0:T(8,128)(2,1)} %base.1, bf16[128,1024]{1,0:T(8,128)(2,1)} %refs_0_.1, ...), custom_call_target="tpu_custom_call" | custom-call | tf_op jit(solution)/shard_map/attention/pallas_call | solution.py:146
  40.8 30.8 %all_to_all.30 = bf16[64,8,512]{2,1,0:T(8,128)(2,1)} all-to-all(bf16[64,8,512]{2,1,0:T(8,128)(2,1)} %bitcast.40), channel_id=1, replica_groups=mesh['ep'=64,'sp'=4] {'ep'}, dimensions={0} | all-to-all | bytes 1048576 | tf_op jit(solution)/shard_map/all_to_all | solution.py:320
  71.6 5.8 %all-to-all-start.1 = ((bf16[64,8,1024]{2,1,0:T(8,128)(2,1)}), bf16[64,8,1024]{2,1,0:T(8,128)(2,1)S(1)}, u32[]{:S(2)}, u32[]{:S(2)}) async-start(bf16[64,8,1024]{2,1,0:T(8,128)(2,1)} %bitcast.39), calls=%async_computation.1 | async-start | bytes 2097152 | tf_op jit(solution)/shard_map/all_to_all | solution.py:320
  77.4 2.3 arrive.3.refs_0_
  79.7 1.2 collective-permute-start.11
  80.9 1.2 collective-permute-start.10
  82.0 2.4 collective-permute-start.9
  84.5 11.7 %collective-permute-done.11.refs_3_ = bf16[64,4096]{1,0:T(8,128)(2,1)S(1)} collective-permute-done((bf16[64,4096]{1,0:T(8,128)(2,1)}, bf16[64,4096]{1,0:T(8,128)(2,1)S(1)}, u32[]{:S(2)}, u32[]{:S(2)}) %collective-permute-start.11) | collective-permute-done | bytes 524320 | tf_op jit(solution)/shard_map/ppermute | solution.py:315
  96.2 10.3 %collective-permute-done.10.refs_2_ = bf16[64,4096]{1,0:T(8,128)(2,1)S(1)} collective-permute-done((bf16[64,4096]{1,0:T(8,128)(2,1)}, bf16[64,4096]{1,0:T(8,128)(2,1)S(1)}, u32[]{:S(2)}, u32[]{:S(2)}) %collective-permute-start.10) | collective-permute-done | bytes 524320 | tf_op jit(solution)/shard_map/ppermute | solution.py:311
  106.5 0.8 copy-done.14
  107.4 10.4 %all-to-all-start.3 = ((bf16[64,8,1024]{2,1,0:T(8,128)(2,1)}), bf16[64,8,1024]{2,1,0:T(8,128)(2,1)S(1)}, u32[]{:S(2)}, u32[]{:S(2)}) async-start(bf16[64,8,1024]{2,1,0:T(8,128)(2,1)} %bitcast.13), calls=%async_computation.3 | async-start | bytes 2097152 | tf_op jit(solution)/shard_map/all_to_all | solution.py:320
  117.8 2.9 arrive.4.refs_0_
  120.7 0.3 collective-permute-start.13
  121.0 2.9 collective-permute-start.16
  123.9 8.6 %expert.3 = (bf16[64,4096]{1,0:T(8,128)(2,1)}, bf16[64,4096]{1,0:T(8,128)(2,1)}, bf16[64,4096]{1,0:T(8,128)(2,1)}, bf16[64,4096]{1,0:T(8,128)(2,1)}) custom-call(bf16[64,4096]{1,0:T(8,128)(2,1)} %arrive.3.refs_0_, bf16[64,4096]{1,0:T(8,128)(2,1)} %copy-done.14, bf16[64,4096]{1,0:T(8,128)(2,1)} %copy-done.13, bf16[64,4096]{1,0:T(8,128)(2,1)} %copy-done.12, ...), custom_call_target="tpu_custom_call" | custom-call | flops 2415919104 | bytes 13631488 | tf_op jit(solution)/shard_map/expert/pallas_call | solution.py:242
  132.6 14.7 %collective-permute-done.13.refs_1_ = bf16[128,4096]{1,0:T(8,128)(2,1)S(1)} collective-permute-done((bf16[128,4096]{1,0:T(8,128)(2,1)}, bf16[128,4096]{1,0:T(8,128)(2,1)S(1)}, u32[]{:S(2)}, u32[]{:S(2)}) %collective-permute-start.13) | collective-permute-done | bytes 1048608 | tf_op jit(solution)/shard_map/ppermute | solution.py:311
  147.3 1.0 copy-done.3
  148.3 3.0 arrive.5.refs_0_
  151.3 3.1 collective-permute-start.19
  154.5 3.2 collective-permute-start.12
  157.7 17.0 %collective-permute-done.17.refs_3_ = bf16[128,4096]{1,0:T(8,128)(2,1)} collective-permute-done((bf16[128,4096]{1,0:T(8,128)(2,1)S(1)}, bf16[128,4096]{1,0:T(8,128)(2,1)}, u32[]{:S(2)}, u32[]{:S(2)}) %collective-permute-start.17) | collective-permute-done | bytes 1048608 | tf_op jit(solution)/shard_map/ppermute | solution.py:311
  174.7 12.2 %expert.4 = (bf16[128,4096]{1,0:T(8,128)(2,1)}, bf16[128,4096]{1,0:T(8,128)(2,1)}, bf16[128,4096]{1,0:T(8,128)(2,1)}, bf16[128,4096]{1,0:T(8,128)(2,1)}) custom-call(bf16[128,4096]{1,0:T(8,128)(2,1)} %arrive.4.refs_0_, bf16[128,4096]{1,0:T(8,128)(2,1)} %copy-done.27, bf16[128,4096]{1,0:T(8,128)(2,1)} %copy-done.28, ...), custom_call_target="tpu_custom_call" | custom-call | flops 4831838208 | bytes 17825792 | tf_op jit(solution)/shard_map/expert/pallas_call | solution.py:242
  186.9 0.3 collective-permute-start.20
  187.2 0.1 add_convert_fusion.2
  187.3 2.1 collective-permute-start.15
  189.5 3.1 collective-permute-start.23
  192.6 10.8 %collective-permute-done.15.last = bf16[64,4096]{1,0:T(8,128)(2,1)S(1)} collective-permute-done((bf16[64,4096]{1,0:T(8,128)(2,1)S(1)}, bf16[64,4096]{1,0:T(8,128)(2,1)S(1)}, u32[]{:S(2)}, u32[]{:S(2)}) %collective-permute-start.15) | collective-permute-done | bytes 524320 | tf_op jit(solution)/shard_map/ppermute | solution.py:311
  203.5 0.8 copy-done.17
  204.3 2.7 leave.3
  206.9 10.4 %all-to-all-start.2 = ((bf16[64,8,512]{2,1,0:T(8,128)(2,1)}), bf16[64,8,512]{2,1,0:T(8,128)(2,1)S(1)}, u32[]{:S(2)}, u32[]{:S(2)}) async-start(bf16[64,8,512]{2,1,0:T(8,128)(2,1)} %bitcast.38), calls=%async_computation.2 | async-start | bytes 1048576 | tf_op jit(solution)/shard_map/all_to_all | solution.py:320
  217.3 0.9 collective-permute-start.18
  218.2 0.2 add_convert_fusion.1
  218.4 2.5 collective-permute-start.21
  221.0 0.5 collective-permute-done.22.refs_2_
  221.5 14.5 %collective-permute-done.23.refs_3_ = bf16[128,4096]{1,0:T(8,128)(2,1)} collective-permute-done((bf16[128,4096]{1,0:T(8,128)(2,1)}, bf16[128,4096]{1,0:T(8,128)(2,1)}, u32[]{:S(2)}, u32[]{:S(2)}) %collective-permute-start.23) | collective-permute-done | bytes 1048608 | tf_op jit(solution)/shard_map/ppermute | solution.py:307
  236.0 12.2 %expert.5 = (bf16[128,4096]{1,0:T(8,128)(2,1)}, bf16[128,4096]{1,0:T(8,128)(2,1)}, bf16[128,4096]{1,0:T(8,128)(2,1)}, bf16[128,4096]{1,0:T(8,128)(2,1)}) custom-call(bf16[128,4096]{1,0:T(8,128)(2,1)} %arrive.5.refs_0_, bf16[128,4096]{1,0:T(8,128)(2,1)} %collective-permute-done.19.refs_1_, bf16[128,4096]{1,0:T(8,128)(2,1)} %collective-permute-done.22.refs_2_, ...), custom_call_target="tpu_custom_call" | custom-call | flops 4831838208 | bytes 17825792 | tf_op jit(solution)/shard_map/expert/pallas_call | solution.py:242
  248.2 6.6 %collective-permute-done.21.last = bf16[128,4096]{1,0:T(8,128)(2,1)S(1)} collective-permute-done((bf16[128,4096]{1,0:T(8,128)(2,1)S(1)}, bf16[128,4096]{1,0:T(8,128)(2,1)S(1)}, u32[]{:S(2)}, u32[]{:S(2)}) %collective-permute-start.21) | collective-permute-done | bytes 1048608 | tf_op jit(solution)/shard_map/ppermute | solution.py:307
  254.8 1.0 copy-done.8
  255.8 3.8 %leave.4 = bf16[512,1024]{1,0:T(8,128)(2,1)} custom-call(bf16[128,4096]{1,0:T(8,128)(2,1)} %get-tuple-element.38.own, bf16[128,4096]{1,0:T(8,128)(2,1)} %copy-done.7, bf16[128,4096]{1,0:T(8,128)(2,1)} %copy-done.8), custom_call_target="tpu_custom_call" | custom-call | tf_op jit(solution)/shard_map/leave/pallas_call | solution.py:192
  259.6 10.6 %all-to-all-start.4 = ((bf16[64,8,1024]{2,1,0:T(8,128)(2,1)}), bf16[64,8,1024]{2,1,0:T(8,128)(2,1)S(1)}, u32[]{:S(2)}, u32[]{:S(2)}) async-start(bf16[64,8,1024]{2,1,0:T(8,128)(2,1)} %bitcast.25), calls=%async_computation.4 | async-start | bytes 2097152 | tf_op jit(solution)/shard_map/all_to_all | solution.py:320
  270.2 4.0 %collective-permute-start.24 = (bf16[128,4096]{1,0:T(8,128)(2,1)}, bf16[128,4096]{1,0:T(8,128)(2,1)S(1)}, u32[]{:S(2)}, u32[]{:S(2)}) collective-permute-start(bf16[128,4096]{1,0:T(8,128)(2,1)} %get-tuple-element.50), channel_id=1, source_target_pairs={{0,1},{1,2},{2,3},{3,0},{4,5},{5,6},{6,7},{7,4},{8,9},{9,10},{10,1... | collective-permute-start | bytes 3145736 | tf_op jit(solution)/shard_map/ppermute | solution.py:307
  274.2 1.5 add_convert_fusion
  275.8 21.4 %collective-permute-done.24.other = bf16[128,4096]{1,0:T(8,128)(2,1)S(1)} collective-permute-done((bf16[128,4096]{1,0:T(8,128)(2,1)}, bf16[128,4096]{1,0:T(8,128)(2,1)S(1)}, u32[]{:S(2)}, u32[]{:S(2)}) %collective-permute-start.24) | collective-permute-done | bytes 1048608 | tf_op jit(solution)/shard_map/ppermute | solution.py:307
  297.1 4.7 %collective-permute-done.26.last = bf16[128,4096]{1,0:T(8,128)(2,1)S(1)} collective-permute-done((bf16[128,4096]{1,0:T(8,128)(2,1)S(1)}, bf16[128,4096]{1,0:T(8,128)(2,1)S(1)}, u32[]{:S(2)}, u32[]{:S(2)}) %collective-permute-start.26) | collective-permute-done | bytes 1048608 | tf_op jit(solution)/shard_map/ppermute | solution.py:311
  301.8 1.0 copy-done.10
  302.8 3.7 %leave.5 = bf16[512,1024]{1,0:T(8,128)(2,1)} custom-call(bf16[128,4096]{1,0:T(8,128)(2,1)} %get-tuple-element.49.own, bf16[128,4096]{1,0:T(8,128)(2,1)} %copy-done.9, bf16[128,4096]{1,0:T(8,128)(2,1)} %copy-done.10), custom_call_target="tpu_custom_call" | custom-call | tf_op jit(solution)/shard_map/leave/pallas_call | solution.py:192
  306.5 39.4 %all_to_all.31 = bf16[64,8,1024]{2,1,0:T(8,128)(2,1)} all-to-all(bf16[64,8,1024]{2,1,0:T(8,128)(2,1)} %bitcast.26), channel_id=1, replica_groups=mesh['ep'=64,'sp'=4] {'ep'}, dimensions={0} | all-to-all | bytes 2097152 | tf_op jit(solution)/shard_map/all_to_all | solution.py:320
  345.9 5.3 %combine.1 = bf16[128,4096]{1,0:T(8,128)(2,1)} custom-call(s32[1]{0:T(128)} %bitcast.sp_ref, s32[2,512]{1,0:T(2,128)} %bitcast.42, s32[2,128]{1,0:T(2,128)} %bitcast.43, bf16[512,512]{1,0:T(8,128)(2,1)} %bitcast.36, bf16[512,1024]{1,0:T(8,128)(2,1)} %bitcast.21, bf16[512,1024]{1,0:T(8,128)(2,1)} %bitcast.22), custom_call_target="tpu_custom_call" | custom-call | tf_op jit(solution)/shard_map/combine/pallas_call | solution.py:295
  (82 shorter events, 0.5 us)
Async XLA Ops:
  0.6 3.0 copy-start
  0.6 15.5 %collective-permute-start = (bf16[128,1024]{1,0:T(8,128)(2,1)}, bf16[128,1024]{1,0:T(8,128)(2,1)S(1)}, u32[]{:S(2)}, u32[]{:S(2)}) collective-permute-start(bf16[128,1024]{1,0:T(8,128)(2,1)} %refs_0_.1), channel_id=1, source_target_pairs={{0,1},{1,2},{2,3},{3,0},{4,5},{5,6},{6,7},{7,4},{8,9},{9,10},{10,1... | collective-permute-start | bytes 786440 | tf_op jit(solution)/shard_map/ppermute | solution.py:307
  2.9 13.5 %collective-permute-start.4 = (bf16[128,1024]{1,0:T(8,128)(2,1)}, bf16[128,1024]{1,0:T(8,128)(2,1)S(1)}, u32[]{:S(2)}, u32[]{:S(2)}) collective-permute-start(bf16[128,1024]{1,0:T(8,128)(2,1)} %refs_4_.1), channel_id=1, source_target_pairs={{0,3},{1,0},{2,1},{3,2},{4,7},{5,4},{6,5},{7,6},{8,11},{9,8},{10,9... | collective-permute-start | bytes 786440 | tf_op jit(solution)/shard_map/ppermute | solution.py:311
  5.0 22.8 %copy-start.15 = (bf16[64,1024]{1,0:T(8,128)(2,1)}, bf16[64,1024]{1,0:T(8,128)(2,1)S(1)}, u32[]{:S(2)}) copy-start(bf16[64,1024]{1,0:T(8,128)(2,1)S(1)} %pad_maximum_fusion.refs_8_) | copy-start | bytes 393220
  5.1 11.0 %collective-permute-start.7 = (bf16[64,1024]{1,0:T(8,128)(2,1)S(1)}, bf16[64,1024]{1,0:T(8,128)(2,1)S(1)}, u32[]{:S(2)}, u32[]{:S(2)}) collective-permute-start(bf16[64,1024]{1,0:T(8,128)(2,1)S(1)} %pad_maximum_fusion.refs_8_), channel_id=1, source_target_pairs={{0,3},{1,0},{2,1},{3,2},{4,7},{5,4},{6,5},{7,6},{8,11},{9,8},{10,9... | collective-permute-start | bytes 393224 | tf_op jit(solution)/shard_map/ppermute | solution.py:311
  5.8 12.5 %collective-permute-start.6 = (bf16[64,1024]{1,0:T(8,128)(2,1)S(1)}, bf16[64,1024]{1,0:T(8,128)(2,1)S(1)}, u32[]{:S(2)}, u32[]{:S(2)}) collective-permute-start(bf16[64,1024]{1,0:T(8,128)(2,1)S(1)} %pad_maximum_fusion.refs_8_), channel_id=1, source_target_pairs={{0,1},{1,2},{2,3},{3,0},{4,5},{5,6},{6,7},{7,4},{8,9},{9,10},{10,1... | collective-permute-start | bytes 393224 | tf_op jit(solution)/shard_map/ppermute | solution.py:307
  8.5 19.3 %collective-permute-start.1 = (bf16[128,1024]{1,0:T(8,128)(2,1)}, bf16[128,1024]{1,0:T(8,128)(2,1)S(1)}, u32[]{:S(2)}, u32[]{:S(2)}) collective-permute-start(bf16[128,1024]{1,0:T(8,128)(2,1)} %refs_0_.1), channel_id=1, source_target_pairs={{0,3},{1,0},{2,1},{3,2},{4,7},{5,4},{6,5},{7,6},{8,11},{9,8},{10,9... | collective-permute-start | bytes 786440 | tf_op jit(solution)/shard_map/ppermute | solution.py:311
  16.1 11.8 %copy-start.24 = (bf16[64,1024]{1,0:T(8,128)(2,1)}, bf16[64,1024]{1,0:T(8,128)(2,1)S(1)}, u32[]{:S(2)}) copy-start(bf16[64,1024]{1,0:T(8,128)(2,1)S(1)} %collective-permute-done.7.refs_10_) | copy-start | bytes 393220
  16.1 11.7 %collective-permute-start.3 = (bf16[128,1024]{1,0:T(8,128)(2,1)}, bf16[128,1024]{1,0:T(8,128)(2,1)S(1)}, u32[]{:S(2)}, u32[]{:S(2)}) collective-permute-start(bf16[128,1024]{1,0:T(8,128)(2,1)} %refs_4_.1), channel_id=1, source_target_pairs={{0,1},{1,2},{2,3},{3,0},{4,5},{5,6},{6,7},{7,4},{8,9},{9,10},{10,1... | collective-permute-start | bytes 786440 | tf_op jit(solution)/shard_map/ppermute | solution.py:307
  16.1 11.8 %copy-start.18 = (bf16[128,1024]{1,0:T(8,128)(2,1)}, bf16[128,1024]{1,0:T(8,128)(2,1)S(1)}, u32[]{:S(2)}) copy-start(bf16[128,1024]{1,0:T(8,128)(2,1)S(1)} %collective-permute-done.refs_1_) | copy-start | bytes 786436
  16.1 11.7 %collective-permute-start.2 = (bf16[128,1024]{1,0:T(8,128)(2,1)S(1)}, bf16[128,1024]{1,0:T(8,128)(2,1)S(1)}, u32[]{:S(2)}, u32[]{:S(2)}) collective-permute-start(bf16[128,1024]{1,0:T(8,128)(2,1)S(1)} %collective-permute-done.refs_1_), channel_id=1, source_target_pairs={{0,1},{1,2},{2,3},{3,0},{4,5},{5,6},{6,7},{7,4},{8,9},{9,10},{10,1... | collective-permute-start | bytes 786440 | tf_op jit(solution)/shard_map/ppermute | solution.py:307
  16.4 11.4 %copy-start.19 = (bf16[128,1024]{1,0:T(8,128)(2,1)}, bf16[128,1024]{1,0:T(8,128)(2,1)S(1)}, u32[]{:S(2)}) copy-start(bf16[128,1024]{1,0:T(8,128)(2,1)S(1)} %collective-permute-done.4.refs_6_) | copy-start | bytes 786436
  16.4 11.4 %collective-permute-start.5 = (bf16[128,1024]{1,0:T(8,128)(2,1)S(1)}, bf16[128,1024]{1,0:T(8,128)(2,1)S(1)}, u32[]{:S(2)}, u32[]{:S(2)}) collective-permute-start(bf16[128,1024]{1,0:T(8,128)(2,1)S(1)} %collective-permute-done.4.refs_6_), channel_id=1, source_target_pairs={{0,3},{1,0},{2,1},{3,2},{4,7},{5,4},{6,5},{7,6},{8,11},{9,8},{10,9... | collective-permute-start | bytes 786440 | tf_op jit(solution)/shard_map/ppermute | solution.py:311
  18.2 9.7 %copy-start.25 = (bf16[64,1024]{1,0:T(8,128)(2,1)}, bf16[64,1024]{1,0:T(8,128)(2,1)S(1)}, u32[]{:S(2)}) copy-start(bf16[64,1024]{1,0:T(8,128)(2,1)S(1)} %collective-permute-done.6.refs_9_) | copy-start | bytes 393220
  18.2 9.6 %collective-permute-start.8 = (bf16[64,1024]{1,0:T(8,128)(2,1)S(1)}, bf16[64,1024]{1,0:T(8,128)(2,1)S(1)}, u32[]{:S(2)}, u32[]{:S(2)}) collective-permute-start(bf16[64,1024]{1,0:T(8,128)(2,1)S(1)} %collective-permute-done.6.refs_9_), channel_id=1, source_target_pairs={{0,1},{1,2},{2,3},{3,0},{4,5},{5,6},{6,7},{7,4},{8,9},{9,10},{10,1... | collective-permute-start | bytes 393224 | tf_op jit(solution)/shard_map/ppermute | solution.py:307
  27.8 0.7 copy-start.26
  27.8 0.8 copy-start.20
  27.8 0.8 copy-start.21
  27.8 0.9 copy-start.22
  27.9 1.0 copy-start.23
  71.6 34.9 %all-to-all-start.1 = ((bf16[64,8,1024]{2,1,0:T(8,128)(2,1)}), bf16[64,8,1024]{2,1,0:T(8,128)(2,1)S(1)}, u32[]{:S(2)}, u32[]{:S(2)}) async-start(bf16[64,8,1024]{2,1,0:T(8,128)(2,1)} %bitcast.39), calls=%async_computation.1 | async-start | bytes 2097152 | tf_op jit(solution)/shard_map/all_to_all | solution.py:320
  79.7 16.5 %collective-permute-start.11 = (bf16[64,4096]{1,0:T(8,128)(2,1)}, bf16[64,4096]{1,0:T(8,128)(2,1)S(1)}, u32[]{:S(2)}, u32[]{:S(2)}) collective-permute-start(bf16[64,4096]{1,0:T(8,128)(2,1)} %arrive.3.refs_0_), channel_id=1, source_target_pairs={{0,2},{1,3},{2,0},{3,1},{4,6},{5,7},{6,4},{7,5},{8,10},{9,11},{10,... | collective-permute-start | bytes 1572872 | tf_op jit(solution)/shard_map/ppermute | solution.py:315
  80.9 25.6 %collective-permute-start.10 = (bf16[64,4096]{1,0:T(8,128)(2,1)}, bf16[64,4096]{1,0:T(8,128)(2,1)S(1)}, u32[]{:S(2)}, u32[]{:S(2)}) collective-permute-start(bf16[64,4096]{1,0:T(8,128)(2,1)} %arrive.3.refs_0_), channel_id=1, source_target_pairs={{0,3},{1,0},{2,1},{3,2},{4,7},{5,4},{6,5},{7,6},{8,11},{9,8},{10,9... | collective-permute-start | bytes 1572872 | tf_op jit(solution)/shard_map/ppermute | solution.py:311
  82.0 24.5 %collective-permute-start.9 = (bf16[64,4096]{1,0:T(8,128)(2,1)}, bf16[64,4096]{1,0:T(8,128)(2,1)S(1)}, u32[]{:S(2)}, u32[]{:S(2)}) collective-permute-start(bf16[64,4096]{1,0:T(8,128)(2,1)} %arrive.3.refs_0_), channel_id=1, source_target_pairs={{0,1},{1,2},{2,3},{3,0},{4,5},{5,6},{6,7},{7,4},{8,9},{9,10},{10,1... | collective-permute-start | bytes 1572872 | tf_op jit(solution)/shard_map/ppermute | solution.py:307
  96.2 24.5 %copy-start.12 = (bf16[64,4096]{1,0:T(8,128)(2,1)}, bf16[64,4096]{1,0:T(8,128)(2,1)S(1)}, u32[]{:S(2)}) copy-start(bf16[64,4096]{1,0:T(8,128)(2,1)S(1)} %collective-permute-done.11.refs_3_) | copy-start | bytes 1572868
  106.5 14.2 %copy-start.13 = (bf16[64,4096]{1,0:T(8,128)(2,1)}, bf16[64,4096]{1,0:T(8,128)(2,1)S(1)}, u32[]{:S(2)}) copy-start(bf16[64,4096]{1,0:T(8,128)(2,1)S(1)} %collective-permute-done.10.refs_2_) | copy-start | bytes 1572868
  106.5 0.8 copy-start.14
  106.5 11.2 %copy-start.2 = (bf16[64,8,1024]{2,1,0:T(8,128)(2,1)}, bf16[64,8,1024]{2,1,0:T(8,128)(2,1)S(1)}, u32[]{:S(2)}) copy-start(bf16[64,8,1024]{2,1,0:T(8,128)(2,1)S(1)} %all-to-all-done.1) | copy-start | bytes 3145732
  107.4 39.9 %all-to-all-start.3 = ((bf16[64,8,1024]{2,1,0:T(8,128)(2,1)}), bf16[64,8,1024]{2,1,0:T(8,128)(2,1)S(1)}, u32[]{:S(2)}, u32[]{:S(2)}) async-start(bf16[64,8,1024]{2,1,0:T(8,128)(2,1)} %bitcast.13), calls=%async_computation.3 | async-start | bytes 2097152 | tf_op jit(solution)/shard_map/all_to_all | solution.py:320
  120.7 26.5 %collective-permute-start.13 = (bf16[128,4096]{1,0:T(8,128)(2,1)}, bf16[128,4096]{1,0:T(8,128)(2,1)S(1)}, u32[]{:S(2)}, u32[]{:S(2)}) collective-permute-start(bf16[128,4096]{1,0:T(8,128)(2,1)} %arrive.4.refs_0_), channel_id=1, source_target_pairs={{0,3},{1,0},{2,1},{3,2},{4,7},{5,4},{6,5},{7,6},{8,11},{9,8},{10,9... | collective-permute-start | bytes 3145736 | tf_op jit(solution)/shard_map/ppermute | solution.py:311
  121.0 30.3 %collective-permute-start.16 = (bf16[128,4096]{1,0:T(8,128)(2,1)}, bf16[128,4096]{1,0:T(8,128)(2,1)S(1)}, u32[]{:S(2)}, u32[]{:S(2)}) collective-permute-start(bf16[128,4096]{1,0:T(8,128)(2,1)} %arrive.4.refs_0_), channel_id=1, source_target_pairs={{0,1},{1,2},{2,3},{3,0},{4,5},{5,6},{6,7},{7,4},{8,9},{9,10},{10,1... | collective-permute-start | bytes 3145736 | tf_op jit(solution)/shard_map/ppermute | solution.py:307
  147.3 27.4 %copy-start.27 = (bf16[128,4096]{1,0:T(8,128)(2,1)}, bf16[128,4096]{1,0:T(8,128)(2,1)S(1)}, u32[]{:S(2)}) copy-start(bf16[128,4096]{1,0:T(8,128)(2,1)S(1)} %collective-permute-done.13.refs_1_) | copy-start | bytes 3145732
  147.3 27.4 %collective-permute-start.17 = (bf16[128,4096]{1,0:T(8,128)(2,1)S(1)}, bf16[128,4096]{1,0:T(8,128)(2,1)}, u32[]{:S(2)}, u32[]{:S(2)}) collective-permute-start(bf16[128,4096]{1,0:T(8,128)(2,1)S(1)} %collective-permute-done.13.refs_1_), channel_id=1, source_target_pairs={{0,3},{1,0},{2,1},{3,2},{4,7},{5,4},{6,5},{7,6},{8,11},{9,8},{10,9... | collective-permute-start | bytes 3145736 | tf_op jit(solution)/shard_map/ppermute | solution.py:311
  147.3 1.0 copy-start.3
  147.3 7.2 %copy-start.30 = (bf16[64,4096]{1,0:T(8,128)(2,1)S(1)}, bf16[64,4096]{1,0:T(8,128)(2,1)}, u32[]{:S(2)}) copy-start(bf16[64,4096]{1,0:T(8,128)(2,1)} %get-tuple-element.36) | copy-start | bytes 1572868
  147.3 7.2 %copy-start.29 = (bf16[64,4096]{1,0:T(8,128)(2,1)S(1)}, bf16[64,4096]{1,0:T(8,128)(2,1)}, u32[]{:S(2)}) copy-start(bf16[64,4096]{1,0:T(8,128)(2,1)} %get-tuple-element.31) | copy-start | bytes 1572868
  151.3 23.4 %copy-start.28 = (bf16[128,4096]{1,0:T(8,128)(2,1)}, bf16[128,4096]{1,0:T(8,128)(2,1)S(1)}, u32[]{:S(2)}) copy-start(bf16[128,4096]{1,0:T(8,128)(2,1)S(1)} %collective-permute-done.16.refs_2_) | copy-start | bytes 3145732
  151.3 35.6 %collective-permute-start.19 = (bf16[128,4096]{1,0:T(8,128)(2,1)}, bf16[128,4096]{1,0:T(8,128)(2,1)}, u32[]{:S(2)}, u32[]{:S(2)}) collective-permute-start(bf16[128,4096]{1,0:T(8,128)(2,1)} %arrive.5.refs_0_), channel_id=1, source_target_pairs={{0,1},{1,2},{2,3},{3,0},{4,5},{5,6},{6,7},{7,4},{8,9},{9,10},{10,1... | collective-permute-start | bytes 3145736 | tf_op jit(solution)/shard_map/ppermute | solution.py:307
  154.5 32.7 %collective-permute-start.14 = (bf16[64,4096]{1,0:T(8,128)(2,1)S(1)}, bf16[64,4096]{1,0:T(8,128)(2,1)S(1)}, u32[]{:S(2)}, u32[]{:S(2)}) collective-permute-start(bf16[64,4096]{1,0:T(8,128)(2,1)S(1)} %copy-done.30), channel_id=1, source_target_pairs={{0,3},{1,0},{2,1},{3,2},{4,7},{5,4},{6,5},{7,6},{8,11},{9,8},{10,9... | collective-permute-start | bytes 1572872 | tf_op jit(solution)/shard_map/ppermute | solution.py:311
  154.5 32.7 %copy-start.11 = (bf16[64,4096]{1,0:T(8,128)(2,1)S(1)}, bf16[64,4096]{1,0:T(8,128)(2,1)}, u32[]{:S(2)}) copy-start(bf16[64,4096]{1,0:T(8,128)(2,1)} %get-tuple-element.32) | copy-start | bytes 1572868
  154.5 38.1 %collective-permute-start.12 = (bf16[64,4096]{1,0:T(8,128)(2,1)S(1)}, bf16[64,4096]{1,0:T(8,128)(2,1)S(1)}, u32[]{:S(2)}, u32[]{:S(2)}) collective-permute-start(bf16[64,4096]{1,0:T(8,128)(2,1)S(1)} %copy-done.29), channel_id=1, source_target_pairs={{0,1},{1,2},{2,3},{3,0},{4,5},{5,6},{6,7},{7,4},{8,9},{9,10},{10,1... | collective-permute-start | bytes 1572872 | tf_op jit(solution)/shard_map/ppermute | solution.py:307
  186.9 31.3 %collective-permute-start.20 = (bf16[128,4096]{1,0:T(8,128)(2,1)}, bf16[128,4096]{1,0:T(8,128)(2,1)S(1)}, u32[]{:S(2)}, u32[]{:S(2)}) collective-permute-start(bf16[128,4096]{1,0:T(8,128)(2,1)} %get-tuple-element.46), channel_id=1, source_target_pairs={{0,1},{1,2},{2,3},{3,0},{4,5},{5,6},{6,7},{7,4},{8,9},{9,10},{10,1... | collective-permute-start | bytes 3145736 | tf_op jit(solution)/shard_map/ppermute | solution.py:307
  187.2 31.0 %copy-start.5 = (bf16[128,4096]{1,0:T(8,128)(2,1)S(1)}, bf16[128,4096]{1,0:T(8,128)(2,1)}, u32[]{:S(2)}) copy-start(bf16[128,4096]{1,0:T(8,128)(2,1)} %get-tuple-element.40) | copy-start | bytes 3145732
  187.3 16.1 %collective-permute-start.15 = (bf16[64,4096]{1,0:T(8,128)(2,1)S(1)}, bf16[64,4096]{1,0:T(8,128)(2,1)S(1)}, u32[]{:S(2)}, u32[]{:S(2)}) collective-permute-start(bf16[64,4096]{1,0:T(8,128)(2,1)S(1)} %add_convert_fusion.2), channel_id=1, source_target_pairs={{0,3},{1,0},{2,1},{3,2},{4,7},{5,4},{6,5},{7,6},{8,11},{9,8},{10,9... | collective-permute-start | bytes 1572872 | tf_op jit(solution)/shard_map/ppermute | solution.py:311
  189.4 32.1 %collective-permute-start.22 = (bf16[128,4096]{1,0:T(8,128)(2,1)}, bf16[128,4096]{1,0:T(8,128)(2,1)}, u32[]{:S(2)}, u32[]{:S(2)}) collective-permute-start(bf16[128,4096]{1,0:T(8,128)(2,1)} %arrive.5.refs_0_), channel_id=1, source_target_pairs={{0,3},{1,0},{2,1},{3,2},{4,7},{5,4},{6,5},{7,6},{8,11},{9,8},{10,9... | collective-permute-start | bytes 3145736 | tf_op jit(solution)/shard_map/ppermute | solution.py:311
  189.5 46.6 %collective-permute-start.23 = (bf16[128,4096]{1,0:T(8,128)(2,1)}, bf16[128,4096]{1,0:T(8,128)(2,1)}, u32[]{:S(2)}, u32[]{:S(2)}) collective-permute-start(bf16[128,4096]{1,0:T(8,128)(2,1)} %collective-permute-done.19.refs_1_), channel_id=1, source_target_pairs={{0,1},{1,2},{2,3},{3,0},{4,5},{5,6},{6,7},{7,4},{8,9},{9,10},{10,1... | collective-permute-start | bytes 3145736 | tf_op jit(solution)/shard_map/ppermute | solution.py:307
  192.6 10.8 %copy-start.16 = (bf16[64,4096]{1,0:T(8,128)(2,1)}, bf16[64,4096]{1,0:T(8,128)(2,1)S(1)}, u32[]{:S(2)}) copy-start(bf16[64,4096]{1,0:T(8,128)(2,1)S(1)} %collective-permute-done.12.other) | copy-start | bytes 1572868
  203.5 0.8 copy-start.17
  206.9 52.6 %all-to-all-start.2 = ((bf16[64,8,512]{2,1,0:T(8,128)(2,1)}), bf16[64,8,512]{2,1,0:T(8,128)(2,1)S(1)}, u32[]{:S(2)}, u32[]{:S(2)}) async-start(bf16[64,8,512]{2,1,0:T(8,128)(2,1)} %bitcast.38), calls=%async_computation.2 | async-start | bytes 1048576 | tf_op jit(solution)/shard_map/all_to_all | solution.py:320
  217.3 30.9 %collective-permute-start.18 = (bf16[128,4096]{1,0:T(8,128)(2,1)}, bf16[128,4096]{1,0:T(8,128)(2,1)S(1)}, u32[]{:S(2)}, u32[]{:S(2)}) collective-permute-start(bf16[128,4096]{1,0:T(8,128)(2,1)} %get-tuple-element.39), channel_id=1, source_target_pairs={{0,3},{1,0},{2,1},{3,2},{4,7},{5,4},{6,5},{7,6},{8,11},{9,8},{10,9... | collective-permute-start | bytes 3145736 | tf_op jit(solution)/shard_map/ppermute | solution.py:311
  218.4 36.4 %collective-permute-start.21 = (bf16[128,4096]{1,0:T(8,128)(2,1)S(1)}, bf16[128,4096]{1,0:T(8,128)(2,1)S(1)}, u32[]{:S(2)}, u32[]{:S(2)}) collective-permute-start(bf16[128,4096]{1,0:T(8,128)(2,1)S(1)} %add_convert_fusion.1), channel_id=1, source_target_pairs={{0,1},{1,2},{2,3},{3,0},{4,5},{5,6},{6,7},{7,4},{8,9},{9,10},{10,1... | collective-permute-start | bytes 3145736 | tf_op jit(solution)/shard_map/ppermute | solution.py:307
  248.2 26.0 %collective-permute-start.25 = (bf16[128,4096]{1,0:T(8,128)(2,1)}, bf16[128,4096]{1,0:T(8,128)(2,1)}, u32[]{:S(2)}, u32[]{:S(2)}) collective-permute-start(bf16[128,4096]{1,0:T(8,128)(2,1)} %get-tuple-element.52), channel_id=1, source_target_pairs={{0,3},{1,0},{2,1},{3,2},{4,7},{5,4},{6,5},{7,6},{8,11},{9,8},{10,9... | collective-permute-start | bytes 3145736 | tf_op jit(solution)/shard_map/ppermute | solution.py:311
  248.2 6.6 %copy-start.7 = (bf16[128,4096]{1,0:T(8,128)(2,1)}, bf16[128,4096]{1,0:T(8,128)(2,1)S(1)}, u32[]{:S(2)}) copy-start(bf16[128,4096]{1,0:T(8,128)(2,1)S(1)} %collective-permute-done.18.other) | copy-start | bytes 3145732
  254.8 1.0 copy-start.8
  259.6 14.6 %copy-start.6 = (bf16[128,4096]{1,0:T(8,128)(2,1)S(1)}, bf16[128,4096]{1,0:T(8,128)(2,1)}, u32[]{:S(2)}) copy-start(bf16[128,4096]{1,0:T(8,128)(2,1)} %get-tuple-element.51) | copy-start | bytes 3145732
  259.6 16.1 %copy-start.4 = (bf16[64,8,512]{2,1,0:T(8,128)(2,1)}, bf16[64,8,512]{2,1,0:T(8,128)(2,1)S(1)}, u32[]{:S(2)}) copy-start(bf16[64,8,512]{2,1,0:T(8,128)(2,1)S(1)} %all-to-all-done.2) | copy-start | bytes 1572868
  259.6 46.9 %all-to-all-start.4 = ((bf16[64,8,1024]{2,1,0:T(8,128)(2,1)}), bf16[64,8,1024]{2,1,0:T(8,128)(2,1)S(1)}, u32[]{:S(2)}, u32[]{:S(2)}) async-start(bf16[64,8,1024]{2,1,0:T(8,128)(2,1)} %bitcast.25), calls=%async_computation.4 | async-start | bytes 2097152 | tf_op jit(solution)/shard_map/all_to_all | solution.py:320
  270.2 26.9 %collective-permute-start.24 = (bf16[128,4096]{1,0:T(8,128)(2,1)}, bf16[128,4096]{1,0:T(8,128)(2,1)S(1)}, u32[]{:S(2)}, u32[]{:S(2)}) collective-permute-start(bf16[128,4096]{1,0:T(8,128)(2,1)} %get-tuple-element.50), channel_id=1, source_target_pairs={{0,1},{1,2},{2,3},{3,0},{4,5},{5,6},{6,7},{7,4},{8,9},{9,10},{10,1... | collective-permute-start | bytes 3145736 | tf_op jit(solution)/shard_map/ppermute | solution.py:307
  275.7 26.1 %collective-permute-start.26 = (bf16[128,4096]{1,0:T(8,128)(2,1)S(1)}, bf16[128,4096]{1,0:T(8,128)(2,1)S(1)}, u32[]{:S(2)}, u32[]{:S(2)}) collective-permute-start(bf16[128,4096]{1,0:T(8,128)(2,1)S(1)} %add_convert_fusion), channel_id=1, source_target_pairs={{0,3},{1,0},{2,1},{3,2},{4,7},{5,4},{6,5},{7,6},{8,11},{9,8},{10,9... | collective-permute-start | bytes 3145736 | tf_op jit(solution)/shard_map/ppermute | solution.py:311
  297.1 4.7 %copy-start.9 = (bf16[128,4096]{1,0:T(8,128)(2,1)}, bf16[128,4096]{1,0:T(8,128)(2,1)S(1)}, u32[]{:S(2)}) copy-start(bf16[128,4096]{1,0:T(8,128)(2,1)S(1)} %collective-permute-done.24.other) | copy-start | bytes 3145732
  301.8 1.0 copy-start.10
  306.5 39.4 %copy-start.1 = (bf16[64,8,1024]{2,1,0:T(8,128)(2,1)}, bf16[64,8,1024]{2,1,0:T(8,128)(2,1)S(1)}, u32[]{:S(2)}) copy-start(bf16[64,8,1024]{2,1,0:T(8,128)(2,1)S(1)} %all-to-all-done.4) | copy-start | bytes 3145732
